TPU v7x, 256 devices: a whole 4x4x8 slice. The times are simulated.
256 devices in a mesh: gx: 8 (over z), gy: 4 (over y), gz: 8 (over x, core).
Axes of the slice: x: 4, y: 4, z: 8, core: 2. Of those that a mesh axis runs over, the one named last changes fastest.
Arguments:
- points: float32 [8192, 3, 128], P(('gx', 'gy', 'gz')), may hold values from -6 to 6
- source: float32 [8192, 128], P(('gx', 'gy', 'gz')), may hold values from -6 to 6
- density: float32 [8192, 128], P(('gx', 'gy', 'gz')), may hold values from -3 to 3
- anterp: bfloat16 [8192, 216, 128], P(('gx', 'gy', 'gz')), may hold values from -0.5 to 0.5
- child_slot: int32 [8192], P(('gx', 'gy', 'gz')), may hold values from 0 to 7, as said below
- child_ops: bfloat16 [8, 216, 216], replicated, may hold values from -0.4375 to 0.4375
- parent: int32 [8192], P(('gx', 'gy', 'gz')), may hold values from 0 to 1023, as said below
- near_list: int32 [8192, 27], P(('gx', 'gy', 'gz')), may hold values from -1 to 8191, as said below
- far_list: int32 [1024, 189], P(('gx', 'gy', 'gz')), may hold values from 0 to 1023
- far_op: int32 [1024, 189], P(('gx', 'gy', 'gz')), may hold values from 0 to 15
- translations: bfloat16 [16, 216, 216], replicated, may hold values from -0.03125 to 0.03125
Outputs:
- density_out: float32 [8192, 128], P(('gx', 'gy', 'gz'))
- potential: float32 [8192, 128], P(('gx', 'gy', 'gz'))
Inputs may be any that keep to these rules, and one draw needn't show every extreme that they name: Every octant has exactly 8 child leaves. Leaf l of device d = l // 32 has a parent octant owned by d or by a device next to d along gz with the same gx and gy index: parent // 4 is d - 1, d or d + 1, never past the ends of gz. `child_slot`: the 8 children of one octant have 8 different positions. `near_list`: row l lists distinct leaves: entry 0 is l itself, then other leaves b with |b - l| <= 13 on devices with the same gx and gy index as l's, then -1 in the remaining slots; at least 9 entries are listed.
All inputs are finite; a program needn't handle non-finite values.
Results may differ from a plain program's by a relative error of at most 0.008.
Values may be sent and summed in bfloat16 or wider, within the bound.
A program may use at most 64 MiB of HBM per device.

v0:
```python
import jax
import jax.numpy as jnp
from jax import lax
from jax.sharding import PartitionSpec as P

OPS = 16
GHOST = 13
ITERS = 2
LEAF_DEV = 32
OCT_DEV = 4


SOFTEN = 0.01
DAMPING = 0.5
FAR_WEIGHT = 0.3
NEAR_WEIGHT = 0.03


def with_halo(array, sides, width):
    for axis, dim in sides:
        count, length = (lax.axis_size(axis), array.shape[dim])
        up = [(i, (i + 1) % count) for i in range(count - 1)]
        down = [(j, i) for i, j in up]
        last = lax.slice_in_dim(array, length - width, length, axis=dim)
        first = lax.slice_in_dim(array, 0, width, axis=dim)
        before = lax.ppermute(last, axis, up)
        after = lax.ppermute(first, axis, down)
        array = jnp.concatenate([before, array, after], axis=dim)
    return array


def kernel_sum(target, near_points, weights):
    squared = jnp.zeros((near_points.shape[0], target.shape[1], near_points.shape[2]), jnp.float32)
    for component in range(3):
        comp_gap = target[component][None, :, None] - near_points[:, component][:, None, :]
        squared = squared + comp_gap * comp_gap
    kernel_tile = 1.0 / jnp.sqrt(squared + SOFTEN)
    return jnp.sum(kernel_tile * weights[:, None, :], axis=(0, 2))


def shards(
    points,
    source,
    density,
    anterp,
    child_slot,
    child_ops,
    parent,
    near_list,
    far_list,
    far_op,
    translations,
):
    highest = lax.Precision.HIGHEST
    device = (lax.axis_index("gx") * lax.axis_size("gy") + lax.axis_index("gy")) * lax.axis_size(
        "gz"
    ) + lax.axis_index("gz")
    padded_points = with_halo(points.astype(jnp.bfloat16), (("gz", 0),), GHOST).astype(points.dtype)
    is_valid = near_list >= 0
    near_slots = jnp.clip(near_list - (device * LEAF_DEV - GHOST), 0, LEAF_DEV + 2 * GHOST - 1)
    parent_slot = parent - (device * OCT_DEV - OCT_DEV)
    op_ids = jnp.arange(OPS, dtype=jnp.int32)
    picked = (far_op[:, :, None] == op_ids[None, None, :]).astype(jnp.bfloat16)
    trans_wide = translations.astype(jnp.float32)
    child_pick = jnp.take(child_ops, child_slot, axis=0)
    density_now = density
    potential = density
    for step in range(ITERS):
        padded_density = with_halo(density_now, (("gz", 0),), GHOST)

        def one_leaf(leaf_id):
            slots_here = near_slots[leaf_id]
            near_points = jnp.take(padded_points, slots_here, axis=0)
            weights = jnp.where(
                is_valid[leaf_id][:, None], jnp.take(padded_density, slots_here, axis=0), 0.0
            )
            return kernel_sum(points[leaf_id], near_points, weights)

        near_field = lax.map(one_leaf, jnp.arange(points.shape[0], dtype=jnp.int32))
        density_b = density_now.astype(jnp.bfloat16)
        leaf_mult = jnp.einsum(
            "lnp,lp->ln", anterp, density_b, preferred_element_type=jnp.float32
        ).astype(jnp.bfloat16)
        contrib = jnp.einsum(
            "lnm,lm->ln", child_pick, leaf_mult, preferred_element_type=jnp.float32
        )
        total_octs = OCT_DEV * lax.axis_size("gx") * lax.axis_size("gy") * lax.axis_size("gz")
        octant_hot = (parent[:, None] == jnp.arange(total_octs, dtype=jnp.int32)[None, :]).astype(
            jnp.float32
        )
        part_table = jnp.dot(octant_hot.T, contrib, precision=highest)
        summed = lax.psum(part_table, ("gx", "gy", "gz"))
        multipole = summed.astype(jnp.bfloat16)
        sources = jnp.take(multipole, far_list, axis=0)
        grouped = jnp.einsum("gko,gkm->gom", picked, sources, preferred_element_type=jnp.float32)
        local_exp = jnp.einsum("onm,gom->gn", trans_wide, grouped, precision=highest).astype(
            jnp.bfloat16
        )
        padded_local = with_halo(local_exp, (("gz", 0),), OCT_DEV)
        parent_local = jnp.take(padded_local, parent_slot, axis=0)
        leaf_local = jnp.einsum(
            "lnm,ln->lm", child_pick, parent_local, preferred_element_type=jnp.float32
        ).astype(jnp.bfloat16)
        far_field = jnp.einsum("lnp,ln->lp", anterp, leaf_local, preferred_element_type=jnp.float32)
        potential = FAR_WEIGHT * far_field + NEAR_WEIGHT * near_field
        density_now = density_now + DAMPING * (jnp.tanh(source - potential) - density_now)
    return (density_now, potential)


def solution(mesh):
    in_specs = (
        P(("gx", "gy", "gz"), None, None),
        P(("gx", "gy", "gz"), None),
        P(("gx", "gy", "gz"), None),
        P(("gx", "gy", "gz"), None, None),
        P(("gx", "gy", "gz")),
        P(),
        P(("gx", "gy", "gz")),
        P(("gx", "gy", "gz"), None),
        P(("gx", "gy", "gz"), None),
        P(("gx", "gy", "gz"), None),
        P(),
    )
    out_specs = (P(("gx", "gy", "gz"), None), P(("gx", "gy", "gz"), None))
    return jax.shard_map(shards, mesh=mesh, in_specs=in_specs, out_specs=out_specs, check_vma=False)
```

profile of v0, /device:TPU:1, one launch (start us, length us, event | category | flops | bytes accessed | tf_op | source)
XLA Modules:
  0.0 549.5 jit_solution(10797074343592703245)
XLA Ops:
  4.2 1.0 fusion.42
  5.3 2.5 gather_fusion.4
  7.8 3.1 fusion.32
  11.5 85.8 %all-reduce.2 = bf16[1024,216]{0,1:T(8,128)(2,1)S(1)} all-reduce(f32[1024,216]{0,1:T(8,128)S(1)} %fusion.13), channel_id=1, replica_groups=mesh['gx'=8,'gy'=4,'gz'=8] {'gx','gy','gz'}, use_global_device_ids=true, to_apply=%region_0.1 | all-reduce | flops 221184 | bytes 1327104 | tf_op jit(solution)/shard_map/psum | solution.py:92
  97.7 2.9 gather_fusion.5
  101.0 2.9 fusion.2
  104.0 2.8 collective-permute-start.1
  106.8 2.8 collective-permute-start
  109.7 1.9 collective-permute-start.3
  111.6 3.6 collective-permute-start.2
  115.3 1.9 collective-permute-start.5
  117.3 3.6 collective-permute-start.4
  121.7 2.7 fusion.29
  125.1 158.3 %while.20 = (s32[]{:T(128)}, f32[32,128]{1,0:T(8,128)S(1)}, s32[32]{0:T(128)S(1)}, f32[32,3,128]{2,1,0:T(4,128)S(1)}, s32[32,27]{1,0:T(8,128)S(1)}, /*index=5*/f...) while((s32[]{:T(128)}, f32[32,128]{1,0:T(8,128)S(1)}, ...), condition=%wide.region_3.8_spmd, body=%wide.region_1.7_spmd.sunk | while | flops 4884391 | bytes 456561 | solution.py:79
  134.1 0.9 multiply_reduce_fusion.4
  139.0 0.9 multiply_reduce_fusion.4
  153.9 0.9 multiply_reduce_fusion.4
  158.8 0.9 multiply_reduce_fusion.4
  163.8 0.9 multiply_reduce_fusion.4
  173.7 0.9 multiply_reduce_fusion.4
  183.6 0.9 multiply_reduce_fusion.4
  283.5 1.0 fusion.40
  284.5 3.1 fusion.25
  288.2 80.1 %all-reduce.3 = bf16[1024,216]{0,1:T(8,128)(2,1)S(1)} all-reduce(f32[1024,216]{0,1:T(8,128)S(1)} %fusion.12), channel_id=1, replica_groups=mesh['gx'=8,'gy'=4,'gz'=8] {'gx','gy','gz'}, use_global_device_ids=true, to_apply=%region_4.9 | all-reduce | flops 221184 | bytes 1327104 | tf_op jit(solution)/shard_map/psum | solution.py:92
  368.5 2.9 gather_fusion.7
  371.8 2.9 fusion.3
  374.7 1.9 collective-permute-start.7
  376.7 3.6 collective-permute-start.6
  380.4 1.9 collective-permute-start.9
  382.3 3.6 collective-permute-start.8
  386.7 2.7 fusion.22
  390.0 158.8 %while.21 = (s32[]{:T(128)}, f32[32,128]{1,0:T(8,128)S(1)}, s32[32]{0:T(128)S(1)}, f32[32,3,128]{2,1,0:T(4,128)S(1)}, s32[32,27]{1,0:T(8,128)S(1)}, /*index=5*/f...) while((s32[]{:T(128)}, f32[32,128]{1,0:T(8,128)S(1)}, ...), condition=%wide.region_7.12_spmd, body=%wide.region_5.11_spmd.sunk | while | flops 4884391 | bytes 456561 | solution.py:79
  (1025 shorter events, 193.4 us)
Async XLA Ops:
  0.6 3.6 copy-start
  0.6 4.6 copy-start.1
  7.8 3.1 copy-start.6
  97.7 3.1 copy-start.7
  100.6 9.0 %copy-start.3 = (f32[32,3,128]{2,0,1:T(8,128)S(1)}, f32[32,3,128]{2,0,1:T(8,128)}, u32[]{:S(2)}) copy-start(f32[32,3,128]{2,0,1:T(8,128)} %param.23) | copy-start | bytes 147460
  100.6 14.7 %copy-start.2 = (f32[32,128]{1,0:T(8,128)S(1)}, f32[32,128]{1,0:T(8,128)}, u32[]{:S(2)}) copy-start(f32[32,128]{1,0:T(8,128)} %param.25) | copy-start | bytes 49156
  100.6 16.6 %copy-start.4 = (s32[32,27]{1,0:T(8,128)S(1)}, s32[32,27]{1,0:T(8,128)}, u32[]{:S(2)}) copy-start(s32[32,27]{1,0:T(8,128)} %param.30) | copy-start | bytes 10372
  104.0 13.3 %collective-permute-start.1 = (bf16[4,216]{1,0:T(4,128)(2,1)S(1)}, bf16[4,216]{1,0:T(4,128)(2,1)S(1)}, u32[]{:S(2)}, u32[]{:S(2)}) collective-permute-start(bf16[4,216]{1,0:T(4,128)(2,1)S(1)} %fusion.2), channel_id=1, source_target_pairs={{1,0},{2,1},{3,2},{4,3},{5,4},{6,5},{7,6},{9,8},{10,9},{11,10},{12... | collective-permute-start | bytes 5192 | tf_op jit(solution)/shard_map/ppermute | solution.py:27
  106.8 14.2 %collective-permute-start = (bf16[4,216]{1,0:T(4,128)(2,1)S(1)}, bf16[4,216]{1,0:T(4,128)(2,1)S(1)}, u32[]{:S(2)}, u32[]{:S(2)}) collective-permute-start(bf16[4,216]{1,0:T(4,128)(2,1)S(1)} %fusion.2), channel_id=1, source_target_pairs={{0,1},{1,2},{2,3},{3,4},{4,5},{5,6},{6,7},{8,9},{9,10},{10,11},{11... | collective-permute-start | bytes 5192 | tf_op jit(solution)/shard_map/ppermute | solution.py:26
  109.7 15.3 %collective-permute-start.3 = (bf16[13,3,128]{2,1,0:T(4,128)(2,1)S(1)}, bf16[13,3,128]{2,1,0:T(4,128)(2,1)S(1)}, u32[]{:S(2)}, u32[]{:S(2)}) collective-permute-start(bf16[13,3,128]{2,1,0:T(4,128)(2,1)S(1)} %get-tuple-element.199), channel_id=1, source_target_pairs={{1,0},{2,1},{3,2},{4,3},{5,4},{6,5},{7,6},{9,8},{10,9},{11,10},{12... | collective-permute-start | bytes 29960 | tf_op jit(solution)/shard_map/ppermute | solution.py:27
  111.6 13.4 %collective-permute-start.2 = (bf16[13,3,128]{2,1,0:T(4,128)(2,1)S(1)}, bf16[13,3,128]{2,1,0:T(4,128)(2,1)S(1)}, u32[]{:S(2)}, u32[]{:S(2)}) collective-permute-start(bf16[13,3,128]{2,1,0:T(4,128)(2,1)S(1)} %get-tuple-element.198), channel_id=1, source_target_pairs={{0,1},{1,2},{2,3},{3,4},{4,5},{5,6},{6,7},{8,9},{9,10},{10,11},{11... | collective-permute-start | bytes 29960 | tf_op jit(solution)/shard_map/ppermute | solution.py:26
  115.3 9.7 %collective-permute-start.5 = (f32[13,128]{1,0:T(8,128)S(1)}, f32[13,128]{1,0:T(8,128)S(1)}, u32[]{:S(2)}, u32[]{:S(2)}) collective-permute-start(f32[13,128]{1,0:T(8,128)S(1)} %get-tuple-element.203), channel_id=1, source_target_pairs={{1,0},{2,1},{3,2},{4,3},{5,4},{6,5},{7,6},{9,8},{10,9},{11,10},{12... | collective-permute-start | bytes 19976 | tf_op jit(solution)/shard_map/ppermute | solution.py:27
  117.3 7.6 %collective-permute-start.4 = (f32[13,128]{1,0:T(8,128)S(1)}, f32[13,128]{1,0:T(8,128)S(1)}, u32[]{:S(2)}, u32[]{:S(2)}) collective-permute-start(f32[13,128]{1,0:T(8,128)S(1)} %get-tuple-element.202), channel_id=1, source_target_pairs={{0,1},{1,2},{2,3},{3,4},{4,5},{5,6},{6,7},{8,9},{9,10},{10,11},{11... | collective-permute-start | bytes 19976 | tf_op jit(solution)/shard_map/ppermute | solution.py:26
  125.1 158.3 %copy-start.5 = (f32[32,128]{1,0:T(8,128)S(1)}, f32[32,128]{1,0:T(8,128)}, u32[]{:S(2)}) copy-start(f32[32,128]{1,0:T(8,128)} %param.24) | copy-start | bytes 49156
  374.7 11.2 %collective-permute-start.7 = (bf16[4,216]{1,0:T(4,128)(2,1)S(1)}, bf16[4,216]{1,0:T(4,128)(2,1)S(1)}, u32[]{:S(2)}, u32[]{:S(2)}) collective-permute-start(bf16[4,216]{1,0:T(4,128)(2,1)S(1)} %fusion.3), channel_id=1, source_target_pairs={{1,0},{2,1},{3,2},{4,3},{5,4},{6,5},{7,6},{9,8},{10,9},{11,10},{12... | collective-permute-start | bytes 5192 | tf_op jit(solution)/shard_map/ppermute | solution.py:27
  376.7 9.3 %collective-permute-start.6 = (bf16[4,216]{1,0:T(4,128)(2,1)S(1)}, bf16[4,216]{1,0:T(4,128)(2,1)S(1)}, u32[]{:S(2)}, u32[]{:S(2)}) collective-permute-start(bf16[4,216]{1,0:T(4,128)(2,1)S(1)} %fusion.3), channel_id=1, source_target_pairs={{0,1},{1,2},{2,3},{3,4},{4,5},{5,6},{6,7},{8,9},{9,10},{10,11},{11... | collective-permute-start | bytes 5192 | tf_op jit(solution)/shard_map/ppermute | solution.py:26
  380.4 9.6 %collective-permute-start.9 = (f32[13,128]{1,0:T(8,128)S(1)}, f32[13,128]{1,0:T(8,128)S(1)}, u32[]{:S(2)}, u32[]{:S(2)}) collective-permute-start(f32[13,128]{1,0:T(8,128)S(1)} %get-tuple-element.201), channel_id=1, source_target_pairs={{1,0},{2,1},{3,2},{4,3},{5,4},{6,5},{7,6},{9,8},{10,9},{11,10},{12... | collective-permute-start | bytes 19976 | tf_op jit(solution)/shard_map/ppermute | solution.py:27
  382.3 7.7 %collective-permute-start.8 = (f32[13,128]{1,0:T(8,128)S(1)}, f32[13,128]{1,0:T(8,128)S(1)}, u32[]{:S(2)}, u32[]{:S(2)}) collective-permute-start(f32[13,128]{1,0:T(8,128)S(1)} %get-tuple-element.200), channel_id=1, source_target_pairs={{0,1},{1,2},{2,3},{3,4},{4,5},{5,6},{6,7},{8,9},{9,10},{10,11},{11... | collective-permute-start | bytes 19976 | tf_op jit(solution)/shard_map/ppermute | solution.py:26
where the time goes:
time: 553 us; the launch traced here: 549 us
  blocking collectives  166 us (30%)
  local copies, waits for them, and re-layouts  132 us (24%)
  loops' own time  127 us (23%)
  other arithmetic  73.2 us (13%)
  starting transfers between devices  27.9 us (5%)
  matrix products  22.3 us (4%)
    psum x2, blocking collectives, shards(): summed = lax.psum(part_table, ('gx', 'gy', 'gz'))  166 us
    another operation x2, loops' own time, shards(): near_field = lax.map(one_leaf, jnp.arange(points.shape[0], dtype=jnp.int32))  127 us
    reduce_sum x64, other arithmetic, kernel_sum(): return jnp.sum(kernel_tile * weights[:, None, :], axis=(0, 2))  56.4 us
    dynamic_slice x64, local copies, waits for them, and re-layouts, shards(): near_field = lax.map(one_leaf, jnp.arange(points.shape[0], dtype=jnp.int32))  39.5 us
    gather x64, local copies, waits for them, and re-layouts, one_leaf(): near_points = jnp.take(padded_points, slots_here, axis=0)  38.8 us
    gather x64, local copies, waits for them, and re-layouts, one_leaf(): jnp.take(padded_density, slots_here, axis=0)  36.5 us
    ppermute x5, starting transfers between devices, with_halo(): before = lax.ppermute(last, axis, up)  17.4 us
  transfers between devices with their start and end apart: 10, of which 0 were waited for; matrix products, arithmetic and copies ran while one was open for 1% of the time, Pallas kernels for 0%

commit v1 on v0

v1 whole, which is shorter than its diff:
```python
import functools

import jax
import jax.numpy as jnp
from jax import lax
from jax.experimental import pallas as pl
from jax.experimental.pallas import tpu as pltpu
from jax.sharding import PartitionSpec as P

OPS = 16
ITERS = 2
SOFTEN = 0.01
DAMPING = 0.5
FAR_WEIGHT = 0.3
NEAR_WEIGHT = 0.03
PTS = 128
NODES = 216
INTER = 189
LEAF_DEV = 32
OCT_DEV = 4
NEAR = 27
HALO = 16
GHOST = 13
PAIRS = LEAF_DEV // 2
WIN = 28
SPAN = WIN * PTS
PAD = LEAF_DEV + 2 * HALO
CHUNKS = SPAN // 256

MESH = pl.DeviceIdType.MESH
F32 = jnp.float32
BF16 = jnp.bfloat16
LAST = (((1,), (1,)), ((), ()))
K_SPLIT = (0, 5, 9, 14, 16)


def iota(shape, dim):
    return lax.broadcasted_iota(jnp.int32, shape, dim)


def dot(a, b):
    return jnp.dot(a, b, preferred_element_type=F32)


def dot_last(a, b):
    return lax.dot_general(a, b, LAST, preferred_element_type=F32)


def split3(v):
    first = v.astype(BF16).astype(F32)
    rest = v - first
    second = rest.astype(BF16).astype(F32)
    third = (rest - second).astype(BF16).astype(F32)
    return first, second, third


def kernel(
    sizes,
    points, source, density, anterp, child_slot, child_ops, parent, near_list, far_list, far_op, translations,
    density_out, potential_out,
    pts_pad, q_pad, fl_prev, fl_next, fo_prev, fo_next, part_send, part_recv, table,
    src_feat, tgt_feat, feat, mask_wide, q_wide, kmat, codes, ops, counts, wide_counts, grouped, near,
    pt_ss, pt_rs, q_ss, q_rs, li_ss, li_rs, pa_ss, pa_rs, z_ss, z_rs, b_ss, b_rs, a_ss, a_rs, c_ss, c_rs,
):
    n_gx, n_gy, n_gz = sizes
    n_x = n_gz // 2
    half = n_gx * n_gy * n_x
    gx, gy, gz = lax.axis_index("gx"), lax.axis_index("gy"), lax.axis_index("gz")
    device = (gx * n_gy + gy) * n_gz + gz
    xx, core = gz // 2, gz % 2
    prev_gz, next_gz = (gz + n_gz - 1) % n_gz, (gz + 1) % n_gz
    fast = gy + core * (xx - gy)
    slow = xx + core * (gy - xx)
    n_fast = n_gy
    base = core * half

    def z_peer(s):
        return ((gx + s) % n_gx, gy, gz)

    def fast_peer(s):
        other = (fast + s) % n_fast
        return (gx, other + core * (gy - other), gz + core * (2 * other + 1 - gz))

    def slow_peer(s):
        other = (slow + s) % n_x
        return (gx, gy + core * (other - gy), 2 * other + core * (gz - 2 * other))

    sibling = (gx, gy, gz + 1 - 2 * core)
    prev_dev, next_dev = (gx, gy, prev_gz), (gx, gy, next_gz)
    outer = (gx, gy, prev_gz + core * (next_gz - prev_gz))

    barrier = pltpu.get_barrier_semaphore()
    peers = [z_peer(s) for s in range(1, n_gx)] + [fast_peer(s) for s in range(1, n_fast)]
    peers += [slow_peer(s) for s in range(1, n_x)] + [sibling, outer]
    for peer in peers:
        pl.semaphore_signal(barrier, inc=1, device_id=peer, device_id_type=MESH)

    pslot = parent[...].reshape(1, LEAF_DEV) - (device * OCT_DEV - OCT_DEV)
    cslot = child_slot[...].reshape(1, LEAF_DEV)
    square = iota((LEAF_DEV, LEAF_DEV), 0) == iota((LEAF_DEV, LEAF_DEV), 1)
    pcol = jnp.sum(jnp.where(square, pslot.astype(F32), 0.0), axis=1, keepdims=True).astype(jnp.int32)
    ccol = jnp.sum(jnp.where(square, cslot.astype(F32), 0.0), axis=1, keepdims=True).astype(jnp.int32)
    row32 = iota((32, LEAF_DEV), 0)
    part_row = 4 * (row32 // 8) + row32 % 4
    row16 = iota((16, 1), 0)

    def remote(src, dst, ss, rs, dev):
        return pltpu.make_async_remote_copy(
            src_ref=src, dst_ref=dst, send_sem=ss, recv_sem=rs, device_id=dev, device_id_type=MESH
        )

    def partial(it, q32):
        q_b = q32.astype(BF16).astype(F32)
        mult = []
        for group in range(2):
            rows = q_b[group * 16 : group * 16 + 16]
            acc = jnp.zeros((16, NODES), F32)
            for r in range(16):
                lhs = jnp.where(row16 == r, rows, 0.0).astype(BF16)
                acc = acc + dot_last(lhs, anterp[group * 16 + r])
            mult.append(acc)
        leaf_mult = jnp.concatenate(mult, axis=0).astype(BF16)
        acc = jnp.zeros((32, NODES), F32)
        for c in range(8):
            hot = jnp.where((part_row == pslot) & (cslot == c), 1.0, 0.0).astype(BF16)
            acc = acc + dot_last(dot(hot, leaf_mult).astype(BF16), child_ops[c])
        zeros = jnp.zeros((8, 256 - NODES), F32)
        for side, lo in ((0, 0), (1, 16), (2, 8)):
            part_send[it, side] = jnp.concatenate([acc[lo : lo + 8], zeros], axis=1)

    def send_partial(it):
        copies = [
            remote(part_send.at[it, 0], part_recv.at[it, 0], pa_ss.at[it, 0], pa_rs.at[it, 0], prev_dev),
            remote(part_send.at[it, 1], part_recv.at[it, 1], pa_ss.at[it, 1], pa_rs.at[it, 1], next_dev),
        ]
        for copy in copies:
            copy.start()
        return copies

    def send_q(it, src):
        copies = [
            remote(src.at[pl.ds(0, HALO)], q_pad.at[it, pl.ds(HALO + LEAF_DEV, HALO)], q_ss.at[it, 0], q_rs.at[it, 0], prev_dev),
            remote(src.at[pl.ds(HALO, HALO)], q_pad.at[it, pl.ds(0, HALO)], q_ss.at[it, 1], q_rs.at[it, 1], next_dev),
        ]
        for copy in copies:
            copy.start()
        return copies

    def own_multipole(it):
        total = part_send[it, 2] + part_recv[it, 0] + part_recv[it, 1]
        low = iota((8, PTS), 0) < 4
        mine = base + (slow * n_fast + fast) * n_gx + gx
        table[it, mine] = jnp.where(low, total[:, :128], total[:, 128:]).astype(BF16)

    def send_z(it):
        mine = base + (slow * n_fast + fast) * n_gx + gx
        block = table.at[it, pl.ds(mine, 1)]
        copies = [remote(block, block, z_ss.at[it, s - 1], z_rs.at[it, s - 1], z_peer(s)) for s in range(1, n_gx)]
        for copy in copies:
            copy.start()
        return copies

    def send_fast(it):
        block = table.at[it, pl.ds(base + (slow * n_fast + fast) * n_gx, n_gx)]
        copies = [remote(block, block, b_ss.at[it, s - 1], b_rs.at[it, s - 1], fast_peer(s)) for s in range(1, n_fast)]
        for copy in copies:
            copy.start()
        return copies

    def send_slow(it):
        block = table.at[it, pl.ds(base + slow * (n_fast * n_gx), n_fast * n_gx)]
        copies = [remote(block, block, a_ss.at[it, s - 1], a_rs.at[it, s - 1], slow_peer(s)) for s in range(1, n_x)]
        for copy in copies:
            copy.start()
        return copies

    def send_core(it):
        block = table.at[it, pl.ds(base, half)]
        copy = remote(block, block, c_ss.at[it], c_rs.at[it], sibling)
        copy.start()
        return [copy]

    def arrive(copies):
        for copy in copies:
            copy.wait_recv()

    def left(copies):
        for copy in copies:
            copy.wait_send()

    def build_source(w0, w1):
        def body(w, carry):
            y = pts_pad[w]
            y1, y2, y3 = split3(y)
            n1, n2, n3 = split3(jnp.sum(y * y, axis=0, keepdims=True))
            feat[0:3, :] = y1
            feat[3:6, :] = y1
            feat[6:9, :] = y2
            feat[9:12, :] = y2
            feat[12:15, :] = y1
            feat[15:18, :] = y3
            feat[18:19, :] = n1
            feat[19:20, :] = n2
            feat[20:21, :] = n3
            feat[21:24, :] = jnp.ones((3, PTS), F32)
            feat[24:32, :] = jnp.zeros((8, PTS), F32)
            src_feat[pl.ds(pl.multiple_of(w * PTS, PTS), PTS), :] = jnp.transpose(feat[...]).astype(BF16)
            return carry

        lax.fori_loop(w0, w1, body, 0)

    def build_target():
        def body(w, carry):
            x = points[w]
            x1, x2, x3 = split3(x)
            n1, n2, n3 = split3(jnp.sum(x * x, axis=0, keepdims=True) + SOFTEN)
            feat[0:3, :] = -2.0 * x1
            feat[3:6, :] = -2.0 * x2
            feat[6:9, :] = -2.0 * x1
            feat[9:12, :] = -2.0 * x2
            feat[12:15, :] = -2.0 * x3
            feat[15:18, :] = -2.0 * x1
            feat[18:21, :] = jnp.ones((3, PTS), F32)
            feat[21:22, :] = n1
            feat[22:23, :] = n2
            feat[23:24, :] = n3
            feat[24:32, :] = jnp.zeros((8, PTS), F32)
            tgt_feat[:, pl.ds(pl.multiple_of(w * PTS, PTS), PTS)] = feat[...].astype(BF16)
            return carry

        lax.fori_loop(0, LEAF_DEV, body, 0)

    def build_mask():
        listed = near_list[...]
        leaf = iota((LEAF_DEV, 1), 0)
        first = device * LEAF_DEV - GHOST + 2 * (leaf // 2)
        slot = jnp.where(listed >= 0, listed - first, -1)
        lane = iota((LEAF_DEV, PTS), 1)
        mask = jnp.zeros((LEAF_DEV, PTS), F32)
        for k in range(NEAR):
            mask = jnp.where(slot[:, k : k + 1] == lane, 1.0, mask)
        r = iota((8 * PAIRS, LEAF_DEV), 0)
        pick = (r // 8 * 2 + (r % 8) // 2 == iota((8 * PAIRS, LEAF_DEV), 1)) & (r % 8 < 4)
        rows = dot(jnp.where(pick, 1.0, 0.0).astype(BF16), mask.astype(BF16)).astype(BF16)
        for c in range(CHUNKS):
            spread = iota((PTS, 256), 0) == 2 * c + iota((PTS, 256), 1) // PTS
            mask_wide[:, c * 256 : c * 256 + 256] = dot(rows, jnp.where(spread, 1.0, 0.0).astype(BF16))

    def build_q(it):
        even = iota((8, PTS), 0) % 2 == 0
        for w in range(PAD):
            row = q_pad[it, w : w + 1, :]
            high = row.astype(BF16).astype(F32)
            q_wide[:, w * PTS : w * PTS + PTS] = jnp.where(even, high, row - high)

    def store_near(t, acc):
        near[pl.ds(2 * t, 1), :] = acc[0:1, :PTS] + acc[1:2, :PTS]
        near[pl.ds(2 * t + 1, 1), :] = acc[2:3, PTS:] + acc[3:4, PTS:]

    def near_lhs(t, c):
        start = pl.multiple_of((2 * t + HALO - GHOST) * PTS + c * 256, PTS)
        rows = pl.ds(pl.multiple_of(8 * t, 8), 8)
        return (mask_wide[rows, c * 256 : c * 256 + 256] * q_wide[:, pl.ds(start, 256)]).astype(BF16)

    def near_first(t0, t1):
        def body(t, carry):
            target = tgt_feat[:, pl.ds(pl.multiple_of(t * 256, 256), 256)]
            acc = jnp.zeros((8, 256), F32)
            for c in range(CHUNKS):
                start = pl.multiple_of((2 * t + HALO - GHOST) * PTS + c * 256, PTS)
                tile = lax.rsqrt(dot(src_feat[pl.ds(start, 256), :], target)).astype(BF16)
                kmat[t, c * 256 : c * 256 + 256, :] = tile
                acc = acc + dot(near_lhs(t, c), tile)
            store_near(t, acc)
            return carry

        lax.fori_loop(t0, t1, body, 0)

    def near_again(t0, t1):
        def body(t, carry):
            acc = jnp.zeros((8, 256), F32)
            for c in range(CHUNKS):
                acc = acc + dot(near_lhs(t, c), kmat[t, c * 256 : c * 256 + 256, :])
            store_near(t, acc)
            return carry

        lax.fori_loop(t0, t1, body, 0)

    def build_codes():
        lg = n_gz.bit_length() - 1
        ly = n_gy.bit_length() - 1
        for row, lists, kinds in ((0, fl_prev, fo_prev), (4, far_list, far_op), (8, fl_next, fo_next)):
            s = lists[...]
            d = s >> 2
            sz = d & (n_gz - 1)
            sy = (d >> lg) & (n_gy - 1)
            sg = d >> (lg + ly)
            sx, sc = sz >> 1, sz & 1
            spot = jnp.where(sc == 0, sx * n_gy + sy, sy * n_x + sx)
            codes[row : row + 4, :] = (sc * half + spot * n_gx + sg) * 4 + (s & 3)
            ops[row : row + 4, :] = kinds[...]

    def build_counts():
        cols = 8 * half
        width = min(256, cols)
        counts[12 * OPS :, :] = jnp.zeros((4 * OPS, cols), BF16)

        def body(g, carry):
            code = codes[pl.ds(g, 1), :]
            kind = jnp.where(iota((OPS, INTER), 0) == ops[pl.ds(g, 1), :], 1.0, 0.0).astype(BF16)
            rows = pl.ds(pl.multiple_of(g * OPS, OPS), OPS)
            for c in range(cols // width):
                hot = jnp.where(iota((width, INTER), 0) + c * width == code, 1.0, 0.0).astype(BF16)
                counts[rows, c * width : (c + 1) * width] = dot_last(kind, hot).astype(BF16)
            return carry

        lax.fori_loop(0, 12, body, 0)
        lane = iota((PTS, 256), 1)
        spread = jnp.where(iota((PTS, 256), 0) == (lane // 8) * 4 + lane % 4, 1.0, 0.0).astype(BF16)
        low = (iota((256, 256), 1) // 4) % 2 == 0
        for c in range(cols // PTS):
            both = dot(counts[:, c * PTS : (c + 1) * PTS], spread)
            wide_counts[0:256, c * 256 : (c + 1) * 256] = jnp.where(low, both, 0.0).astype(BF16)
            wide_counts[256:512, c * 256 : (c + 1) * 256] = jnp.where(low, 0.0, both).astype(BF16)

    def far_field(it):
        blocks = table[it].reshape(16 * half, PTS)
        grouped[...] = dot(wide_counts[...], blocks)
        acc = jnp.zeros((32, NODES), F32)
        for o in range(OPS):
            full = jnp.concatenate(
                [grouped[pl.ds(o, 16, stride=16), :], grouped[pl.ds(256 + o, 16, stride=16), :]], axis=1
            )[:, :NODES]
            high = full.astype(BF16)
            low = (full - high.astype(F32)).astype(BF16)
            acc = acc + dot_last(jnp.concatenate([high, low], axis=0), translations[o])
        local_exp = (acc[:16] + acc[16:]).astype(BF16)
        lane16 = iota((LEAF_DEV, 16), 1)
        acc = jnp.zeros((LEAF_DEV, NODES), F32)
        for c in range(8):
            hot = jnp.where((pcol == lane16) & (ccol == c), 1.0, 0.0).astype(BF16)
            acc = acc + dot(dot(hot, local_exp).astype(BF16), child_ops[c])
        leaf_local = acc.astype(BF16).astype(F32)
        fields = []
        for group in range(2):
            rows = leaf_local[group * 16 : group * 16 + 16]
            acc = jnp.zeros((16, PTS), F32)
            for r in range(16):
                lhs = jnp.where(row16 == r, rows, 0.0).astype(BF16)
                acc = acc + dot(lhs, anterp[group * 16 + r])
            fields.append(acc)
        return jnp.concatenate(fields, axis=0)

    own = pl.ds(HALO, LEAF_DEV)
    q_pad[0, HALO : HALO + LEAF_DEV, :] = density[...]
    partial(0, density[...])
    pl.semaphore_wait(barrier, len(peers))
    sent = send_partial(0)
    parts = sent
    halo = [
        remote(points.at[pl.ds(0, HALO)], pts_pad.at[pl.ds(HALO + LEAF_DEV, HALO)], pt_ss.at[0], pt_rs.at[0], prev_dev),
        remote(points.at[pl.ds(HALO, HALO)], pts_pad.at[pl.ds(0, HALO)], pt_ss.at[1], pt_rs.at[1], next_dev),
        remote(far_list, fl_next, li_ss.at[0], li_rs.at[0], prev_dev),
        remote(far_list, fl_prev, li_ss.at[1], li_rs.at[1], next_dev),
        remote(far_op, fo_next, li_ss.at[2], li_rs.at[2], prev_dev),
        remote(far_op, fo_prev, li_ss.at[3], li_rs.at[3], next_dev),
    ]
    for copy in halo:
        copy.start()
    halo = halo + send_q(0, density)
    sent = sent + halo
    pts_pad[own] = points[...]
    build_target()
    arrive(parts)
    own_multipole(0)
    copies = send_z(0)
    sent = sent + copies
    build_source(HALO, HALO + LEAF_DEV)
    build_mask()
    arrive(halo)
    build_source(0, HALO)
    build_source(HALO + LEAF_DEV, PAD)
    build_q(0)
    build_codes()
    near_first(K_SPLIT[0], K_SPLIT[1])
    arrive(copies)
    copies = send_fast(0)
    sent = sent + copies
    near_first(K_SPLIT[1], K_SPLIT[2])
    arrive(copies)
    copies = send_slow(0)
    sent = sent + copies
    build_counts()
    near_first(K_SPLIT[2], K_SPLIT[3])
    arrive(copies)
    copies = send_core(0)
    sent = sent + copies
    near_first(K_SPLIT[3], K_SPLIT[4])
    arrive(copies)
    potential = FAR_WEIGHT * far_field(0) + NEAR_WEIGHT * near[...]
    q = density[...]
    q = q + DAMPING * (jnp.tanh(source[...] - potential) - q)

    q_pad[1, HALO : HALO + LEAF_DEV, :] = q
    halo = send_q(1, q_pad.at[1, own])
    partial(1, q)
    parts = send_partial(1)
    sent = sent + halo + parts
    arrive(halo)
    build_q(1)
    arrive(parts)
    own_multipole(1)
    copies = send_z(1)
    sent = sent + copies
    near_again(0, PAIRS // 2)
    arrive(copies)
    copies = send_fast(1)
    sent = sent + copies
    near_again(PAIRS // 2, PAIRS)
    arrive(copies)
    copies = send_slow(1)
    sent = sent + copies
    arrive(copies)
    copies = send_core(1)
    sent = sent + copies
    arrive(copies)
    potential = FAR_WEIGHT * far_field(1) + NEAR_WEIGHT * near[...]
    q = q_pad[1, HALO : HALO + LEAF_DEV, :]
    potential_out[...] = potential
    density_out[...] = q + DAMPING * (jnp.tanh(source[...] - potential) - q)
    left(sent)


def solution(mesh):
    sizes = (mesh.shape["gx"], mesh.shape["gy"], mesh.shape["gz"])
    n_gx, n_gy, n_gz = sizes
    blocks = n_gx * n_gy * n_gz
    cols = 4 * blocks
    vmem = pl.BlockSpec(memory_space=pltpu.VMEM)
    dma = pltpu.SemaphoreType.DMA

    def shards(*args):
        return pl.pallas_call(
            functools.partial(kernel, sizes),
            out_shape=(jax.ShapeDtypeStruct((LEAF_DEV, PTS), F32),) * 2,
            in_specs=[vmem] * 11,
            out_specs=(vmem, vmem),
            scratch_shapes=[
                pltpu.VMEM((PAD, 3, PTS), F32),
                pltpu.VMEM((2, PAD, PTS), F32),
                pltpu.VMEM((OCT_DEV, INTER), jnp.int32),
                pltpu.VMEM((OCT_DEV, INTER), jnp.int32),
                pltpu.VMEM((OCT_DEV, INTER), jnp.int32),
                pltpu.VMEM((OCT_DEV, INTER), jnp.int32),
                pltpu.VMEM((2, 3, 8, 256), F32),
                pltpu.VMEM((2, 2, 8, 256), F32),
                pltpu.VMEM((2, blocks, 8, PTS), BF16),
                pltpu.VMEM((PAD * PTS, 32), BF16),
                pltpu.VMEM((32, LEAF_DEV * PTS), BF16),
                pltpu.VMEM((32, PTS), F32),
                pltpu.VMEM((8 * PAIRS, SPAN), F32),
                pltpu.VMEM((8, PAD * PTS), F32),
                pltpu.VMEM((PAIRS, SPAN, 256), BF16),
                pltpu.VMEM((16, INTER), jnp.int32),
                pltpu.VMEM((16, INTER), jnp.int32),
                pltpu.VMEM((256, cols), BF16),
                pltpu.VMEM((512, 2 * cols), BF16),
                pltpu.VMEM((512, PTS), F32),
                pltpu.VMEM((LEAF_DEV, PTS), F32),
                dma((2,)), dma((2,)), dma((2, 2)), dma((2, 2)), dma((4,)), dma((4,)), dma((2, 2)), dma((2, 2)),
                dma((2, n_gx - 1)), dma((2, n_gx - 1)), dma((2, n_gy - 1)), dma((2, n_gy - 1)),
                dma((2, n_gz // 2 - 1)), dma((2, n_gz // 2 - 1)), dma((2,)), dma((2,)),
            ],
            compiler_params=pltpu.CompilerParams(
                collective_id=0, has_side_effects=True, vmem_limit_bytes=60 * 1024 * 1024
            ),
        )(*args)

    whole = ("gx", "gy", "gz")
    in_specs = (
        P(whole, None, None),
        P(whole, None),
        P(whole, None),
        P(whole, None, None),
        P(whole),
        P(),
        P(whole),
        P(whole, None),
        P(whole, None),
        P(whole, None),
        P(),
    )
    out_specs = (P(whole, None), P(whole, None))
    return jax.shard_map(shards, mesh=mesh, in_specs=in_specs, out_specs=out_specs, check_vma=False)
```

time: 553 us -> 88.9 us (0.16)
  blocking collectives: 166 us -> 0 us
  local copies, waits for them, and re-layouts: 132 us -> 4.1 us
  loops' own time: 127 us -> 0 us
  Pallas kernels: 0 us -> 83.8 us
  other arithmetic: 73.2 us -> 0 us
  starting transfers between devices: 27.9 us -> 0 us
  matrix products: 22.3 us -> 0 us
    psum x2 -> x0, blocking collectives: 166 us -> none  [shards(): summed = lax.psum(part_table, ('gx', 'gy', 'gz'))]
    another operation x2 -> x0, loops' own time: 127 us -> none  [shards(): near_field = lax.map(one_leaf, jnp.arange(points.shape[0], dtype=jnp.int32))]
    gather x135 -> x0, local copies, waits for them, and re-layouts: 85 us -> none  [the longest x64 38.8 us: one_leaf(): near_points = jnp.take(padded_points, slots_here, axis=0)]
    pallas_call x0 -> x1, Pallas kernels: none -> 83.8 us  [shards(): pl.pallas_call(functools.partial(kernel, sizes), out_shape=(jax.ShapeDtyp...]
    reduce_sum x64 -> x0, other arithmetic: 56.4 us -> none  [kernel_sum(): return jnp.sum(kernel_tile * weights[:, None, :], axis=(0, 2))]
    dynamic_slice x128 -> x0, local copies, waits for them, and re-layouts: 40.1 us -> none  [the longest x64 39.5 us: shards(): near_field = lax.map(one_leaf, jnp.arange(points.shape[0], dtype=jnp.int32))]
    ppermute x10 -> x0, starting transfers between devices: 27.9 us -> none  [the longest x5 17.4 us: with_halo(): before = lax.ppermute(last, axis, up)]
    dot_general x14 -> x0, matrix products: 22.3 us -> none  [the longest x2 6.21 us: shards(): jnp.einsum('lnm,lm->ln', child_pick, leaf_mult, preferred_element_type=jn...]
  transfers between devices with their start and end apart: 10 -> 0, of which waited for: 0 -> 0; matrix products, arithmetic and copies ran while one was open for 1% -> 0% of each run, Pallas kernels for 0% -> 0%
where the time goes in v1:
time: 88.9 us; the launch traced here: 88.6 us
  Pallas kernels  83.8 us (94%)
  local copies, waits for them, and re-layouts  4.1 us (5%)
    pallas_call x1, Pallas kernels, shards(): pl.pallas_call(functools.partial(kernel, sizes), out_shape=(jax.ShapeDtyp...  83.8 us
    unnamed x3, local copies, waits for them, and re-layouts  4.1 us

profile of v1, /device:TPU:1, one launch (start us, length us, event | category | flops | bytes accessed | tf_op | source)
XLA Modules:
  0.0 88.6 jit_solution(4043827302135118543)
XLA Ops:
  0.6 1.5 %copy.13.points = f32[32,3,128]{2,1,0:T(4,128)} copy(f32[32,3,128]{2,0,1:T(8,128)} %param.11) | data formatting | bytes 98304 | tf_op args[0]
  2.1 83.8 %shard_map.122 = (f32[32,128]{1,0:T(8,128)}, f32[32,128]{1,0:T(8,128)}) custom-call(f32[32,3,128]{2,1,0:T(4,128)} %copy.13.points, f32[32,128]{1,0:T(8,128)} %source.1, f32[32,128]{1,0:T(8,128)} %density.1, bf16[32,216,128]{2,1,0:T(8,128)(2,1)} %anterp.1, s32[32]{0:T(128)} %child_slot.1, bf16[8,216,216]{2,1,0:T(8,128)(2,1)} %child_ops.1, s32[32]{0:T(128)} %parent.1, ...), custom_call_target="tpu_custom_call" | custom-call | tf_op jit(solution)/shard_map/pallas_call | solution.py:443
  85.9 1.3 %copy.16 = f32[32,128]{1,0:T(8,128)} copy(f32[32,128]{1,0:T(8,128)} %get-tuple-element.4) | data formatting | bytes 32768
  87.3 1.3 %copy.17 = f32[32,128]{1,0:T(8,128)} copy(f32[32,128]{1,0:T(8,128)} %get-tuple-element.5) | data formatting | bytes 32768

commit v2 on v1

v2 whole, which is shorter than its diff:
```python
import functools

import jax
import jax.numpy as jnp
from jax import lax
from jax.experimental import pallas as pl
from jax.experimental.pallas import tpu as pltpu
from jax.sharding import PartitionSpec as P

OPS = 16
ITERS = 2
SOFTEN = 0.01
DAMPING = 0.5
FAR_WEIGHT = 0.3
NEAR_WEIGHT = 0.03
PTS = 128
NODES = 216
INTER = 189
LEAF_DEV = 32
OCT_DEV = 4
NEAR = 27
HALO = 16
GHOST = 13
PAIRS = LEAF_DEV // 2
WIN = 28
SPAN = WIN * PTS
PAD = LEAF_DEV + 2 * HALO
CHUNKS = SPAN // 256

MESH = pl.DeviceIdType.MESH
F32 = jnp.float32
BF16 = jnp.bfloat16
LAST = (((1,), (1,)), ((), ()))
K_SPLIT = (0, 5, 9, 14, 16)


def iota(shape, dim):
    return lax.broadcasted_iota(jnp.int32, shape, dim)


def dot(a, b):
    return jnp.dot(a, b, preferred_element_type=F32)


def dot_last(a, b):
    return lax.dot_general(a, b, LAST, preferred_element_type=F32)


def split3(v):
    first = v.astype(BF16).astype(F32)
    rest = v - first
    second = rest.astype(BF16).astype(F32)
    third = (rest - second).astype(BF16).astype(F32)
    return first, second, third


def kernel(
    sizes,
    points, source, density, anterp, child_slot, child_ops, parent, near_list, far_list, far_op, translations,
    result,
    pts_pad, q_pad, fl_prev, fl_next, fo_prev, fo_next, part_out, part_in, table,
    src_feat, tgt_feat, feat, mask_wide, q_wide, kmat, codes, ops, counts, grouped, near, trans,
    tr_sem, pt_ss, pt_rs, q_ss, q_rs, li_ss, li_rs, pa_ss, pa_rs, z_ss, z_rs, b_ss, b_rs, a_ss, a_rs, c_ss, c_rs,
):
    n_gx, n_gy, n_gz = sizes
    n_x = n_gz // 2
    gx, gy, gz = lax.axis_index("gx"), lax.axis_index("gy"), lax.axis_index("gz")
    device = (gx * n_gy + gy) * n_gz + gz
    xx, core = gz // 2, gz % 2
    prev_gz, next_gz = (gz + n_gz - 1) % n_gz, (gz + 1) % n_gz
    fast = gy + core * (xx - gy)
    slow = xx + core * (gy - xx)
    n_side = n_gy

    def z_peer(s):
        return ((gx + s) % n_gx, gy, gz)

    def fast_peer(s):
        other = (fast + s) % n_side
        return (gx, other + core * (gy - other), gz + core * (2 * other + 1 - gz))

    def slow_peer(s):
        other = (slow + s) % n_side
        return (gx, gy + core * (other - gy), 2 * other + core * (gz - 2 * other))

    sibling = (gx, gy, gz + 1 - 2 * core)
    prev_dev, next_dev = (gx, gy, prev_gz), (gx, gy, next_gz)
    outer = (gx, gy, prev_gz + core * (next_gz - prev_gz))
    outer_x = (xx + n_x - 1 + 2 * core) % n_x

    def spot(a, b):
        return (a + core * (b - a)) * n_side + b + core * (a - b)

    def piece(it, i, j):
        return table.at[it, core, spot((slow + i) % n_side, (fast + j) % n_side)]

    barrier = pltpu.get_barrier_semaphore()
    peers = [z_peer(s) for s in range(1, n_gx)] + [fast_peer(s) for s in range(1, n_side)]
    peers += [slow_peer(s) for s in range(1, n_side)] + [sibling, outer]
    for peer in peers:
        pl.semaphore_signal(barrier, inc=1, device_id=peer, device_id_type=MESH)

    load_trans = pltpu.make_async_copy(translations, trans, tr_sem)
    load_trans.start()
    pslot = parent[...].reshape(1, LEAF_DEV) - (device * OCT_DEV - OCT_DEV)
    cslot = child_slot[...].reshape(1, LEAF_DEV)
    square = iota((LEAF_DEV, LEAF_DEV), 0) == iota((LEAF_DEV, LEAF_DEV), 1)
    pcol = jnp.sum(jnp.where(square, pslot.astype(F32), 0.0), axis=1, keepdims=True).astype(jnp.int32)
    ccol = jnp.sum(jnp.where(square, cslot.astype(F32), 0.0), axis=1, keepdims=True).astype(jnp.int32)
    chip_slot = parent[...].reshape(1, LEAF_DEV) - (device - core) * OCT_DEV
    part_row = iota((16, LEAF_DEV), 0)
    part_row = jnp.where(part_row < 8, part_row, part_row - 16 + 16 * core)
    row16 = iota((16, 1), 0)

    def remote(src, dst, ss, rs, dev):
        return pltpu.make_async_remote_copy(
            src_ref=src, dst_ref=dst, send_sem=ss, recv_sem=rs, device_id=dev, device_id_type=MESH
        )

    def partial(it, q32):
        q_b = q32.astype(BF16).astype(F32)
        mult = []
        for group in range(2):
            rows = q_b[group * 16 : group * 16 + 16]
            acc = jnp.zeros((16, NODES), F32)
            for r in range(16):
                lhs = jnp.where(row16 == r, rows, 0.0).astype(BF16)
                acc = acc + dot_last(lhs, anterp[group * 16 + r])
            mult.append(acc)
        leaf_mult = jnp.concatenate(mult, axis=0).astype(BF16)
        acc = jnp.zeros((16, NODES), F32)
        for c in range(8):
            hot = jnp.where((part_row == chip_slot) & (cslot == c), 1.0, 0.0).astype(BF16)
            acc = acc + dot_last(dot(hot, leaf_mult).astype(BF16), child_ops[c])
        low = acc[:, :PTS]
        high = jnp.concatenate([acc[:, PTS:], jnp.zeros((16, 256 - NODES), F32)], axis=1)
        part_out[it, 0] = jnp.where(core == 0, high[:8], low[:8])
        part_out[it, 1] = low[8:]
        part_out[it, 2] = high[8:]
        part_out[it, 3] = jnp.where(core == 0, low[:8], high[:8])

    def send_partial(it):
        copies = [remote(part_out.at[it, 0], part_in.at[it, 0], pa_ss.at[it, 0], pa_rs.at[it, 0], sibling)]
        for h in range(2):
            copies.append(
                remote(
                    part_out.at[it, 1 + h], part_in.at[it, 2 - core], pa_ss.at[it, 1 + h], pa_rs.at[it, 2 - core],
                    (gx, gy, 2 * outer_x + h),
                )
            )
        for copy in copies:
            copy.start()
        return copies

    def own_multipole(it):
        for k in range(3):
            remote(part_out.at[it, k], part_in.at[it, k], pa_ss.at[it, k], pa_rs.at[it, k], sibling).wait_recv()
        total = part_out[it, 3] + part_in[it, 0] + part_in[it, 1] + part_in[it, 2]
        table[it, core, spot(slow, fast), gx] = total.astype(BF16)

    def send_q(it, src):
        copies = [
            remote(src.at[pl.ds(0, HALO)], q_pad.at[it, pl.ds(HALO + LEAF_DEV, HALO)], q_ss.at[it, 0], q_rs.at[it, 0], prev_dev),
            remote(src.at[pl.ds(HALO, HALO)], q_pad.at[it, pl.ds(0, HALO)], q_ss.at[it, 1], q_rs.at[it, 1], next_dev),
        ]
        for copy in copies:
            copy.start()
        return copies

    def send_z(it):
        block = table.at[it, core, spot(slow, fast), pl.ds(gx, 1)]
        copies = [remote(block, block, z_ss.at[it, s - 1], z_rs.at[it, s - 1], z_peer(s)) for s in range(1, n_gx)]
        for copy in copies:
            copy.start()
        return copies

    def fast_copies(it):
        block = piece(it, 0, 0)
        return [remote(block, block, b_ss.at[it, s - 1], b_rs.at[it, s - 1], fast_peer(s)) for s in range(1, n_side)]

    def slow_copies(it, j):
        block = piece(it, 0, j)
        return [
            remote(block, block, a_ss.at[it, s - 1, j], a_rs.at[it, s - 1, j], slow_peer(s)) for s in range(1, n_side)
        ]

    def core_copy(it, i, j):
        block = piece(it, i, j)
        return remote(block, block, c_ss.at[it, i, j], c_rs.at[it, i, j], sibling)

    def gather_start(it):
        fasts, slows, cores = fast_copies(it), slow_copies(it, 0), core_copy(it, 0, 0)
        copies = fasts + slows + [cores]
        for copy in copies:
            copy.start()
        return copies

    def gather_middle(it):
        fasts = fast_copies(it)
        sent = []
        for j in range(1, n_side):
            fasts[n_side - j - 1].wait_recv()
            copies = slow_copies(it, j) + [core_copy(it, 0, j)]
            for copy in copies:
                copy.start()
            sent += copies
        return sent

    def gather_end(it):
        sent = []
        for j in range(n_side):
            slows = slow_copies(it, j)
            for i in range(1, n_side):
                slows[n_side - i - 1].wait_recv()
                copy = core_copy(it, i, j)
                copy.start()
                sent.append(copy)
        return sent

    def gather_wait(it):
        for i in range(n_side):
            for j in range(n_side):
                core_copy(it, i, j).wait_recv()

    def arrive(copies):
        for copy in copies:
            copy.wait_recv()

    def left(copies):
        for copy in copies:
            copy.wait_send()

    def planes(rows, values):
        for f, value in enumerate(values):
            feat[f * PAD : f * PAD + rows, :] = value

    def build_source():
        parts = [split3(pts_pad[c]) for c in range(3)]
        norm = split3(pts_pad[0] * pts_pad[0] + pts_pad[1] * pts_pad[1] + pts_pad[2] * pts_pad[2])
        values = [parts[c][k] for k in (0, 0, 1, 1, 0, 2) for c in range(3)] + list(norm) + [jnp.ones((PAD, PTS), F32)] * 3
        planes(PAD, values)

        def body(w, carry):
            tile = jnp.transpose(feat[pl.ds(w, 32, stride=PAD), :]).astype(BF16)
            src_feat[pl.ds(pl.multiple_of(w * PTS, PTS), PTS), :] = tile
            return carry

        lax.fori_loop(2, PAD - 2, body, 0, unroll=4)

    def build_target():
        parts = [[-2.0 * v for v in split3(points[c])] for c in range(3)]
        norm = split3(points[0] * points[0] + points[1] * points[1] + points[2] * points[2] + SOFTEN)
        values = [parts[c][k] for k in (0, 1, 0, 1, 2, 0) for c in range(3)] + [jnp.ones((LEAF_DEV, PTS), F32)] * 3 + list(norm)
        planes(LEAF_DEV, values)
        feat[24 * PAD :, :] = jnp.zeros((8 * PAD, PTS), F32)

        def body(w, carry):
            tgt_feat[:, pl.ds(pl.multiple_of(w * PTS, PTS), PTS)] = feat[pl.ds(w, 32, stride=PAD), :].astype(BF16)
            return carry

        lax.fori_loop(0, LEAF_DEV, body, 0, unroll=4)

    def build_mask():
        listed = near_list[...]
        leaf = iota((LEAF_DEV, 1), 0)
        first = device * LEAF_DEV - GHOST + 2 * (leaf // 2)
        slot = jnp.where(listed >= 0, listed - first, -1)
        lane = iota((LEAF_DEV, PTS), 1)
        mask = jnp.zeros((LEAF_DEV, PTS), F32)
        for k in range(NEAR):
            mask = jnp.where(slot[:, k : k + 1] == lane, 1.0, mask)
        r = iota((8 * PAIRS, LEAF_DEV), 0)
        pick = (r // 8 * 2 + (r % 8) // 2 == iota((8 * PAIRS, LEAF_DEV), 1)) & (r % 8 < 4)
        rows = dot(jnp.where(pick, 1.0, 0.0).astype(BF16), mask.astype(BF16)).astype(BF16)
        for c in range(CHUNKS):
            spread = iota((PTS, 256), 0) == 2 * c + iota((PTS, 256), 1) // PTS
            mask_wide[:, c * 256 : c * 256 + 256] = dot(rows, jnp.where(spread, 1.0, 0.0).astype(BF16))

    def build_q(it):
        even = iota((8, PTS), 0) % 2 == 0
        for w in range(PAD):
            row = q_pad[it, w : w + 1, :]
            high = row.astype(BF16).astype(F32)
            q_wide[:, w * PTS : w * PTS + PTS] = jnp.where(even, high, row - high)

    def store_near(t, acc):
        near[pl.ds(2 * t, 1), :] = acc[0:1, :PTS] + acc[1:2, :PTS]
        near[pl.ds(2 * t + 1, 1), :] = acc[2:3, PTS:] + acc[3:4, PTS:]

    def near_lhs(t, c):
        start = pl.multiple_of((2 * t + HALO - GHOST) * PTS + c * 256, PTS)
        rows = pl.ds(pl.multiple_of(8 * t, 8), 8)
        return (mask_wide[rows, c * 256 : c * 256 + 256] * q_wide[:, pl.ds(start, 256)]).astype(BF16)

    def near_first(t0, t1):
        def body(t, carry):
            target = tgt_feat[:, pl.ds(pl.multiple_of(t * 256, 256), 256)]
            start = pl.multiple_of((2 * t + HALO - GHOST) * PTS, PTS)
            kmat[t] = lax.rsqrt(dot(src_feat[pl.ds(start, SPAN), :], target).astype(BF16))
            return carry

        lax.fori_loop(t0, t1, body, 0)
        near_again(t0, t1)

    def near_again(t0, t1):
        def body(t, carry):
            acc = jnp.zeros((8, 256), F32)
            for c in range(CHUNKS):
                acc = acc + dot(near_lhs(t, c), kmat[t, c * 256 : c * 256 + 256, :])
            store_near(t, acc)
            return carry

        lax.fori_loop(t0, t1, body, 0)

    def build_codes():
        lg = n_gz.bit_length() - 1
        ly = n_gy.bit_length() - 1
        for row, lists, kinds in ((0, fl_prev, fo_prev), (4, far_list, far_op), (8, fl_next, fo_next)):
            s = lists[...]
            d = s >> 2
            sx = (d & (n_gz - 1)) >> 1
            sy = (d >> lg) & (n_gy - 1)
            sg = d >> (lg + ly)
            codes[row : row + 4, :] = ((sx * n_gy + sy) * n_gx + sg) * 8 + (s & 7)
            ops[row : row + 4, :] = kinds[...]

    def build_counts():
        cols = 8 * n_side * n_side * n_gx
        width = min(256, cols)
        for start in (12 * OPS, 28 * OPS):
            grouped[start : start + 4 * OPS, :] = jnp.zeros((4 * OPS, PTS), F32)

        def body(g, carry):
            code = codes[pl.ds(g, 1), :]
            kind = jnp.where(iota((OPS, INTER), 0) == ops[pl.ds(g, 1), :], 1.0, 0.0).astype(BF16)
            rows = pl.ds(pl.multiple_of(g * OPS, OPS), OPS)
            for c in range(cols // width):
                hot = jnp.where(iota((width, INTER), 0) + c * width == code, 1.0, 0.0).astype(BF16)
                counts[rows, c * width : (c + 1) * width] = dot_last(kind, hot).astype(BF16)
            return carry

        lax.fori_loop(0, 12, body, 0)
    def far_field(it):
        cols = 8 * n_side * n_side * n_gx
        blocks = jnp.concatenate([table[it, 0].reshape(cols, PTS), table[it, 1].reshape(cols, PTS)], axis=1)
        both = dot(counts[...], blocks)
        grouped[0 : 12 * OPS, :] = both[:, :PTS]
        grouped[16 * OPS : 28 * OPS, :] = both[:, PTS:]
        acc = jnp.zeros((32, NODES), F32)
        for o in range(OPS):
            full = jnp.concatenate(
                [grouped[pl.ds(o, 16, stride=16), :], grouped[pl.ds(256 + o, 16, stride=16), :]], axis=1
            )[:, :NODES]
            high = full.astype(BF16)
            low = (full - high.astype(F32)).astype(BF16)
            acc = acc + dot_last(jnp.concatenate([high, low], axis=0), trans[o])
        local_exp = (acc[:16] + acc[16:]).astype(BF16)
        lane16 = iota((LEAF_DEV, 16), 1)
        acc = jnp.zeros((LEAF_DEV, NODES), F32)
        for c in range(8):
            hot = jnp.where((pcol == lane16) & (ccol == c), 1.0, 0.0).astype(BF16)
            acc = acc + dot(dot(hot, local_exp).astype(BF16), child_ops[c])
        leaf_local = acc.astype(BF16).astype(F32)
        fields = []
        for group in range(2):
            rows = leaf_local[group * 16 : group * 16 + 16]
            acc = jnp.zeros((16, PTS), F32)
            for r in range(16):
                lhs = jnp.where(row16 == r, rows, 0.0).astype(BF16)
                acc = acc + dot(lhs, anterp[group * 16 + r])
            fields.append(acc)
        return jnp.concatenate(fields, axis=0)

    own = pl.ds(HALO, LEAF_DEV)
    first, last = pl.ds(0, HALO), pl.ds(HALO, HALO)
    after = pl.ds(HALO + LEAF_DEV, HALO)
    q_pad[0, HALO : HALO + LEAF_DEV, :] = density[...]
    partial(0, density[...])
    pl.semaphore_wait(barrier, len(peers))
    sent = send_partial(0)
    halo = [
        remote(points.at[:, first], pts_pad.at[:, after], pt_ss.at[0], pt_rs.at[0], prev_dev),
        remote(points.at[:, last], pts_pad.at[:, first], pt_ss.at[1], pt_rs.at[1], next_dev),
    ]
    for copy in halo:
        copy.start()
    halo = halo + send_q(0, density)
    lists = [
        remote(far_list, fl_next, li_ss.at[0], li_rs.at[0], prev_dev),
        remote(far_list, fl_prev, li_ss.at[1], li_rs.at[1], next_dev),
        remote(far_op, fo_next, li_ss.at[2], li_rs.at[2], prev_dev),
        remote(far_op, fo_prev, li_ss.at[3], li_rs.at[3], next_dev),
    ]
    for copy in lists:
        copy.start()
    sent = sent + halo + lists
    for c in range(3):
        pts_pad[c, HALO : HALO + LEAF_DEV, :] = points[c]
    build_target()
    own_multipole(0)
    copies = send_z(0)
    sent = sent + copies
    build_mask()
    arrive(halo)
    build_source()
    build_q(0)
    near_first(K_SPLIT[0], K_SPLIT[1])
    arrive(copies)
    sent = sent + gather_start(0)
    near_first(K_SPLIT[1], K_SPLIT[2])
    sent = sent + gather_middle(0)
    arrive(lists)
    build_codes()
    build_counts()
    near_first(K_SPLIT[2], K_SPLIT[3])
    sent = sent + gather_end(0)
    near_first(K_SPLIT[3], K_SPLIT[4])
    load_trans.wait()
    gather_wait(0)
    potential = FAR_WEIGHT * far_field(0) + NEAR_WEIGHT * near[...]
    q = density[...]
    q = q + DAMPING * (jnp.tanh(source[...] - potential) - q)

    q_pad[1, HALO : HALO + LEAF_DEV, :] = q
    halo = send_q(1, q_pad.at[1, own])
    partial(1, q)
    sent = sent + halo + send_partial(1)
    arrive(halo)
    build_q(1)
    own_multipole(1)
    copies = send_z(1)
    sent = sent + copies
    near_again(0, PAIRS // 2)
    arrive(copies)
    sent = sent + gather_start(1)
    near_again(PAIRS // 2, PAIRS)
    sent = sent + gather_middle(1)
    sent = sent + gather_end(1)
    gather_wait(1)
    potential = FAR_WEIGHT * far_field(1) + NEAR_WEIGHT * near[...]
    q = q_pad[1, HALO : HALO + LEAF_DEV, :]
    result[0] = q + DAMPING * (jnp.tanh(source[...] - potential) - q)
    result[1] = potential
    left(sent)


def solution(mesh):
    sizes = (mesh.shape["gx"], mesh.shape["gy"], mesh.shape["gz"])
    n_gx, n_gy, n_gz = sizes
    n_side = n_gy
    cols = 4 * n_gx * n_gy * n_gz
    vmem = pl.BlockSpec(memory_space=pltpu.VMEM)
    dma = pltpu.SemaphoreType.DMA

    def shards(points, *args):
        out = pl.pallas_call(
            functools.partial(kernel, sizes),
            out_shape=jax.ShapeDtypeStruct((2, LEAF_DEV, PTS), F32),
            in_specs=[vmem] * 10 + [pl.BlockSpec(memory_space=pl.ANY)],
            out_specs=vmem,
            scratch_shapes=[
                pltpu.VMEM((3, PAD, PTS), F32),
                pltpu.VMEM((2, PAD, PTS), F32),
                pltpu.VMEM((OCT_DEV, INTER), jnp.int32),
                pltpu.VMEM((OCT_DEV, INTER), jnp.int32),
                pltpu.VMEM((OCT_DEV, INTER), jnp.int32),
                pltpu.VMEM((OCT_DEV, INTER), jnp.int32),
                pltpu.VMEM((2, 4, 8, PTS), F32),
                pltpu.VMEM((2, 3, 8, PTS), F32),
                pltpu.VMEM((2, 2, n_side * n_side, n_gx, 8, PTS), BF16),
                pltpu.VMEM((PAD * PTS, 32), BF16),
                pltpu.VMEM((32, LEAF_DEV * PTS), BF16),
                pltpu.VMEM((32 * PAD, PTS), F32),
                pltpu.VMEM((8 * PAIRS, SPAN), F32),
                pltpu.VMEM((8, PAD * PTS), F32),
                pltpu.VMEM((PAIRS, SPAN, 256), BF16),
                pltpu.VMEM((16, INTER), jnp.int32),
                pltpu.VMEM((16, INTER), jnp.int32),
                pltpu.VMEM((12 * OPS, cols), BF16),
                pltpu.VMEM((32 * OPS, PTS), F32),
                pltpu.VMEM((LEAF_DEV, PTS), F32),
                pltpu.VMEM((OPS, NODES, NODES), BF16),
                dma, dma((2,)), dma((2,)), dma((2, 2)), dma((2, 2)), dma((4,)), dma((4,)), dma((2, 3)), dma((2, 3)),
                dma((2, n_gx - 1)), dma((2, n_gx - 1)), dma((2, n_side - 1)), dma((2, n_side - 1)),
                dma((2, n_side - 1, n_side)), dma((2, n_side - 1, n_side)), dma((2, n_side, n_side)), dma((2, n_side, n_side)),
            ],
            compiler_params=pltpu.CompilerParams(
                collective_id=0, has_side_effects=True, vmem_limit_bytes=60 * 1024 * 1024
            ),
        )(jnp.transpose(points, (1, 0, 2)), *args)
        return out[0], out[1]

    whole = ("gx", "gy", "gz")
    in_specs = (
        P(whole, None, None),
        P(whole, None),
        P(whole, None),
        P(whole, None, None),
        P(whole),
        P(),
        P(whole),
        P(whole, None),
        P(whole, None),
        P(whole, None),
        P(),
    )
    out_specs = (P(whole, None), P(whole, None))
    return jax.shard_map(shards, mesh=mesh, in_specs=in_specs, out_specs=out_specs, check_vma=False)
```

time: 88.9 us -> 65.4 us (0.74)
  Pallas kernels: 83.8 us -> 63.2 us
  local copies, waits for them, and re-layouts: 4.1 us -> 1.35 us
    pallas_call x1, Pallas kernels: 83.8 us -> 63.2 us  [shards(): pl.pallas_call(functools.partial(kernel, sizes), out_shape=jax.ShapeDtype...]
    unnamed x3 -> x0, local copies, waits for them, and re-layouts: 4.1 us -> none
    squeeze x0 -> x1, local copies, waits for them, and re-layouts: none -> 1.35 us  [shards(): return (out[0], out[1])]
where the time goes in v2:
time: 65.4 us; the launch traced here: 65.2 us
  Pallas kernels  63.2 us (97%)
  local copies, waits for them, and re-layouts  1.35 us (2%)
    pallas_call x1, Pallas kernels, shards(): pl.pallas_call(functools.partial(kernel, sizes), out_shape=jax.ShapeDtype...  63.2 us
    squeeze x1, local copies, waits for them, and re-layouts, shards(): return (out[0], out[1])  1.35 us

profile of v2, /device:TPU:1, one launch (start us, length us, event | category | flops | bytes accessed | tf_op | source)
XLA Modules:
  0.0 65.2 jit_solution(7061144266334645869)
XLA Ops:
  0.6 63.2 %shard_map.122 = f32[2,32,128]{2,1,0:T(8,128)} custom-call(f32[3,32,128]{2,1,0:T(8,128)} %bitcast.5, f32[32,128]{1,0:T(8,128)} %source.1, f32[32,128]{1,0:T(8,128)} %density.1, bf16[32,216,128]{2,1,0:T(8,128)(2,1)} %anterp.1, s32[32]{0:T(128)} %child_slot.1, bf16[8,216,216]{2,1,0:T(8,128)(2,1)} %child_ops.1, s32[32]{0:T(128)} %parent.1, s32[32,27]{1,0:T(8,128)} %near_list.1, ...), custom_call_target="tpu_custom_call" | custom-call | tf_op jit(solution)/shard_map/pallas_call | solution.py:456
  63.8 1.3 %slice_bitcast_fusion = (f32[32,128]{1,0:T(8,128)}, f32[32,128]{1,0:T(8,128)}) fusion(f32[2,32,128]{2,1,0:T(8,128)} %shard_map.122), kind=kLoop, calls=%fused_computation | loop fusion | bytes 65536 | tf_op jit(solution)/shard_map/squeeze | solution.py:491

commit v3 on v2

--- a/solution.py
+++ b/solution.py
@@ -20,18 +20,18 @@
 OCT_DEV = 4
 NEAR = 27
 HALO = 16
-GHOST = 13
 PAIRS = LEAF_DEV // 2
-WIN = 28
-SPAN = WIN * PTS
+SIDE = 7
+CHUNKS = 2 * SIDE + 1
+SPAN = CHUNKS * 256
+UPPER = SIDE * 256 + PTS
 PAD = LEAF_DEV + 2 * HALO
-CHUNKS = SPAN // 256
 
 MESH = pl.DeviceIdType.MESH
 F32 = jnp.float32
 BF16 = jnp.bfloat16
 LAST = (((1,), (1,)), ((), ()))
-K_SPLIT = (0, 5, 9, 14, 16)
+K_SPLIT = (0, 0, 8, 14, 16)
 
 
 def iota(shape, dim):
@@ -59,8 +59,8 @@
     points, source, density, anterp, child_slot, child_ops, parent, near_list, far_list, far_op, translations,
     result,
     pts_pad, q_pad, fl_prev, fl_next, fo_prev, fo_next, part_out, part_in, table,
-    src_feat, tgt_feat, feat, mask_wide, q_wide, kmat, codes, ops, counts, grouped, near, trans,
-    tr_sem, pt_ss, pt_rs, q_ss, q_rs, li_ss, li_rs, pa_ss, pa_rs, z_ss, z_rs, b_ss, b_rs, a_ss, a_rs, c_ss, c_rs,
+    src_feat, tgt_feat, feat, mask_wide, q_wide, kmat, codes, ops, counts, grouped, near, trans, rows_of,
+    tr_sem, pt_ss, pt_rs, q_ss, q_rs, li_ss, li_rs, pa_ss, pa_rs, z_ss, z_rs, a_ss, a_rs, c_ss, c_rs,
 ):
     n_gx, n_gy, n_gz = sizes
     n_x = n_gz // 2
@@ -75,13 +75,12 @@
     def z_peer(s):
         return ((gx + s) % n_gx, gy, gz)
 
-    def fast_peer(s):
-        other = (fast + s) % n_side
-        return (gx, other + core * (gy - other), gz + core * (2 * other + 1 - gz))
-
-    def slow_peer(s):
-        other = (slow + s) % n_side
-        return (gx, gy + core * (other - gy), 2 * other + core * (gz - 2 * other))
+    offsets = [(i, j) for i in range(n_side) for j in range(n_side) if i or j]
+    offsets.sort(key=lambda o: min(o[0], n_side - o[0]) + min(o[1], n_side - o[1]))
+
+    def side_peer(i, j):
+        a, b = (slow + i) % n_side, (fast + j) % n_side
+        return (gx, b + core * (a - b), 2 * (a + core * (b - a)) + core)
 
     sibling = (gx, gy, gz + 1 - 2 * core)
     prev_dev, next_dev = (gx, gy, prev_gz), (gx, gy, next_gz)
@@ -95,8 +94,7 @@
         return table.at[it, core, spot((slow + i) % n_side, (fast + j) % n_side)]
 
     barrier = pltpu.get_barrier_semaphore()
-    peers = [z_peer(s) for s in range(1, n_gx)] + [fast_peer(s) for s in range(1, n_side)]
-    peers += [slow_peer(s) for s in range(1, n_side)] + [sibling, outer]
+    peers = [z_peer(s) for s in range(1, n_gx)] + [side_peer(i, j) for i, j in offsets] + [sibling, outer]
     for peer in peers:
         pl.semaphore_signal(barrier, inc=1, device_id=peer, device_id_type=MESH)
 
@@ -123,9 +121,10 @@
         for group in range(2):
             rows = q_b[group * 16 : group * 16 + 16]
             acc = jnp.zeros((16, NODES), F32)
-            for r in range(16):
-                lhs = jnp.where(row16 == r, rows, 0.0).astype(BF16)
-                acc = acc + dot_last(lhs, anterp[group * 16 + r])
+            for r in range(0, 16, 2):
+                lhs = jnp.concatenate([jnp.where(row16 == r + k, rows, 0.0) for k in range(2)], axis=1).astype(BF16)
+                both = jnp.concatenate([anterp[group * 16 + r], anterp[group * 16 + r + 1]], axis=1)
+                acc = acc + dot_last(lhs, both)
             mult.append(acc)
         leaf_mult = jnp.concatenate(mult, axis=0).astype(BF16)
         acc = jnp.zeros((16, NODES), F32)
@@ -174,48 +173,34 @@
             copy.start()
         return copies
 
-    def fast_copies(it):
+    def side_copy(it, i, j):
         block = piece(it, 0, 0)
-        return [remote(block, block, b_ss.at[it, s - 1], b_rs.at[it, s - 1], fast_peer(s)) for s in range(1, n_side)]
-
-    def slow_copies(it, j):
-        block = piece(it, 0, j)
-        return [
-            remote(block, block, a_ss.at[it, s - 1, j], a_rs.at[it, s - 1, j], slow_peer(s)) for s in range(1, n_side)
-        ]
+        return remote(block, block, a_ss.at[it, i, j], a_rs.at[it, i, j], side_peer(i, j))
 
     def core_copy(it, i, j):
         block = piece(it, i, j)
         return remote(block, block, c_ss.at[it, i, j], c_rs.at[it, i, j], sibling)
 
     def gather_start(it):
-        fasts, slows, cores = fast_copies(it), slow_copies(it, 0), core_copy(it, 0, 0)
-        copies = fasts + slows + [cores]
+        copies = [side_copy(it, i, j) for i, j in offsets[::-1]] + [core_copy(it, 0, 0)]
         for copy in copies:
             copy.start()
         return copies
 
+    def forward(it, batch):
+        sent = []
+        for i, j in batch:
+            side_copy(it, i, j).wait_recv()
+            copy = core_copy(it, (n_side - i) % n_side, (n_side - j) % n_side)
+            copy.start()
+            sent.append(copy)
+        return sent
+
     def gather_middle(it):
-        fasts = fast_copies(it)
-        sent = []
-        for j in range(1, n_side):
-            fasts[n_side - j - 1].wait_recv()
-            copies = slow_copies(it, j) + [core_copy(it, 0, j)]
-            for copy in copies:
-                copy.start()
-            sent += copies
-        return sent
+        return forward(it, offsets[: len(offsets) // 2])
 
     def gather_end(it):
-        sent = []
-        for j in range(n_side):
-            slows = slow_copies(it, j)
-            for i in range(1, n_side):
-                slows[n_side - i - 1].wait_recv()
-                copy = core_copy(it, i, j)
-                copy.start()
-                sent.append(copy)
-        return sent
+        return forward(it, offsets[len(offsets) // 2 :])
 
     def gather_wait(it):
         for i in range(n_side):
@@ -248,22 +233,22 @@
         lax.fori_loop(2, PAD - 2, body, 0, unroll=4)
 
     def build_target():
-        parts = [[-2.0 * v for v in split3(points[c])] for c in range(3)]
-        norm = split3(points[0] * points[0] + points[1] * points[1] + points[2] * points[2] + SOFTEN)
-        values = [parts[c][k] for k in (0, 1, 0, 1, 2, 0) for c in range(3)] + [jnp.ones((LEAF_DEV, PTS), F32)] * 3 + list(norm)
-        planes(LEAF_DEV, values)
+        parts = [[-2.0 * v for v in split3(pts_pad[c])] for c in range(3)]
+        norm = split3(pts_pad[0] * pts_pad[0] + pts_pad[1] * pts_pad[1] + pts_pad[2] * pts_pad[2] + SOFTEN)
+        values = [parts[c][k] for k in (0, 1, 0, 1, 2, 0) for c in range(3)] + [jnp.ones((PAD, PTS), F32)] * 3 + list(norm)
+        planes(PAD, values)
         feat[24 * PAD :, :] = jnp.zeros((8 * PAD, PTS), F32)
 
         def body(w, carry):
             tgt_feat[:, pl.ds(pl.multiple_of(w * PTS, PTS), PTS)] = feat[pl.ds(w, 32, stride=PAD), :].astype(BF16)
             return carry
 
-        lax.fori_loop(0, LEAF_DEV, body, 0, unroll=4)
+        lax.fori_loop(0, HALO + LEAF_DEV, body, 0, unroll=6)
 
     def build_mask():
         listed = near_list[...]
         leaf = iota((LEAF_DEV, 1), 0)
-        first = device * LEAF_DEV - GHOST + 2 * (leaf // 2)
+        first = device * LEAF_DEV - 2 * SIDE + 2 * (leaf // 2)
         slot = jnp.where(listed >= 0, listed - first, -1)
         lane = iota((LEAF_DEV, PTS), 1)
         mask = jnp.zeros((LEAF_DEV, PTS), F32)
@@ -288,29 +273,40 @@
         near[pl.ds(2 * t + 1, 1), :] = acc[2:3, PTS:] + acc[3:4, PTS:]
 
     def near_lhs(t, c):
-        start = pl.multiple_of((2 * t + HALO - GHOST) * PTS + c * 256, PTS)
+        start = pl.multiple_of((t + HALO // 2 - SIDE + c) * 256, 256)
         rows = pl.ds(pl.multiple_of(8 * t, 8), 8)
         return (mask_wide[rows, c * 256 : c * 256 + 256] * q_wide[:, pl.ds(start, 256)]).astype(BF16)
 
-    def near_first(t0, t1):
-        def body(t, carry):
-            target = tgt_feat[:, pl.ds(pl.multiple_of(t * 256, 256), 256)]
-            start = pl.multiple_of((2 * t + HALO - GHOST) * PTS, PTS)
-            kmat[t] = lax.rsqrt(dot(src_feat[pl.ds(start, SPAN), :], target).astype(BF16))
-            return carry
-
-        lax.fori_loop(t0, t1, body, 0)
-        near_again(t0, t1)
+    def build_halo():
+        for e in range(SIDE):
+            target = tgt_feat[:, (e + 1) * 256 : (e + 2) * 256]
+            tile = dot(src_feat[HALO * PTS : HALO * PTS + (e + 1) * 256 - PTS, :], target)
+            kmat[e, (SIDE - e) * 256 :, :] = lax.rsqrt(tile.astype(BF16))
 
     def near_again(t0, t1):
         def body(t, carry):
             acc = jnp.zeros((8, 256), F32)
-            for c in range(CHUNKS):
-                acc = acc + dot(near_lhs(t, c), kmat[t, c * 256 : c * 256 + 256, :])
+            for o in range(SIDE):
+                acc = acc + dot(near_lhs(t, SIDE + o), kmat[t + SIDE, o * 256 : o * 256 + 256, :])
+            acc = acc + dot(near_lhs(t, 2 * SIDE)[:, :PTS], kmat[t + SIDE, SIDE * 256 :, :])
+            for o in range(1, SIDE):
+                acc = acc + dot_last(near_lhs(t, SIDE - o), kmat[t + SIDE - o, o * 256 : o * 256 + 256, :])
+            edge = dot_last(near_lhs(t, 0), kmat[t, SIDE * 256 :, :])
+            acc = acc + jnp.concatenate([edge, jnp.zeros((8, PTS), F32)], axis=1)
             store_near(t, acc)
             return carry
 
-        lax.fori_loop(t0, t1, body, 0)
+        lax.fori_loop(t0, t1, body, 0, unroll=2)
+
+    def near_first(t0, t1):
+        def body(t, carry):
+            start = pl.multiple_of((t + HALO // 2) * 256, 256)
+            target = tgt_feat[:, pl.ds(start, 256)]
+            kmat[t + SIDE] = lax.rsqrt(dot(src_feat[pl.ds(start, UPPER), :], target).astype(BF16))
+            return carry
+
+        lax.fori_loop(t0, t1, body, 0, unroll=2)
+        near_again(t0, t1)
 
     def build_codes():
         lg = n_gz.bit_length() - 1
@@ -327,20 +323,24 @@
     def build_counts():
         cols = 8 * n_side * n_side * n_gx
         width = min(256, cols)
+        rows_of[...] = iota((cols, INTER), 0).astype(jnp.int16)
         for start in (12 * OPS, 28 * OPS):
             grouped[start : start + 4 * OPS, :] = jnp.zeros((4 * OPS, PTS), F32)
 
         def body(g, carry):
-            code = codes[pl.ds(g, 1), :]
+            code16 = jnp.broadcast_to(codes[pl.ds(g, 1), :], (16, INTER)).astype(jnp.int16)
+            code16 = jnp.broadcast_to(code16[:1], (width, INTER))
+            one16, zero16 = jnp.ones((width, INTER), BF16), jnp.zeros((width, INTER), BF16)
             kind = jnp.where(iota((OPS, INTER), 0) == ops[pl.ds(g, 1), :], 1.0, 0.0).astype(BF16)
             rows = pl.ds(pl.multiple_of(g * OPS, OPS), OPS)
             for c in range(cols // width):
-                hot = jnp.where(iota((width, INTER), 0) + c * width == code, 1.0, 0.0).astype(BF16)
+                hot = jnp.where(rows_of[c * width : (c + 1) * width, :] == code16, one16, zero16)
                 counts[rows, c * width : (c + 1) * width] = dot_last(kind, hot).astype(BF16)
             return carry
 
         lax.fori_loop(0, 12, body, 0)
     def far_field(it):
+        gather_wait(it)
         cols = 8 * n_side * n_side * n_gx
         blocks = jnp.concatenate([table[it, 0].reshape(cols, PTS), table[it, 1].reshape(cols, PTS)], axis=1)
         both = dot(counts[...], blocks)
@@ -360,14 +360,15 @@
         for c in range(8):
             hot = jnp.where((pcol == lane16) & (ccol == c), 1.0, 0.0).astype(BF16)
             acc = acc + dot(dot(hot, local_exp).astype(BF16), child_ops[c])
-        leaf_local = acc.astype(BF16).astype(F32)
+        leaf_local = acc.astype(BF16)
         fields = []
         for group in range(2):
             rows = leaf_local[group * 16 : group * 16 + 16]
             acc = jnp.zeros((16, PTS), F32)
-            for r in range(16):
-                lhs = jnp.where(row16 == r, rows, 0.0).astype(BF16)
-                acc = acc + dot(lhs, anterp[group * 16 + r])
+            for r in range(0, 16, 2):
+                both = jnp.concatenate([anterp[group * 16 + r], anterp[group * 16 + r + 1]], axis=1)
+                pair = dot(rows, both)
+                acc = jnp.where(row16 == r, pair[:, :PTS], jnp.where(row16 == r + 1, pair[:, PTS:], acc))
             fields.append(acc)
         return jnp.concatenate(fields, axis=0)
 
@@ -396,13 +397,14 @@
     sent = sent + halo + lists
     for c in range(3):
         pts_pad[c, HALO : HALO + LEAF_DEV, :] = points[c]
-    build_target()
+    build_mask()
     own_multipole(0)
     copies = send_z(0)
     sent = sent + copies
-    build_mask()
     arrive(halo)
+    build_target()
     build_source()
+    build_halo()
     build_q(0)
     near_first(K_SPLIT[0], K_SPLIT[1])
     arrive(copies)
@@ -416,7 +418,6 @@
     sent = sent + gather_end(0)
     near_first(K_SPLIT[3], K_SPLIT[4])
     load_trans.wait()
-    gather_wait(0)
     potential = FAR_WEIGHT * far_field(0) + NEAR_WEIGHT * near[...]
     q = density[...]
     q = q + DAMPING * (jnp.tanh(source[...] - potential) - q)
@@ -436,7 +437,6 @@
     near_again(PAIRS // 2, PAIRS)
     sent = sent + gather_middle(1)
     sent = sent + gather_end(1)
-    gather_wait(1)
     potential = FAR_WEIGHT * far_field(1) + NEAR_WEIGHT * near[...]
     q = q_pad[1, HALO : HALO + LEAF_DEV, :]
     result[0] = q + DAMPING * (jnp.tanh(source[...] - potential) - q)
@@ -469,20 +469,21 @@
                 pltpu.VMEM((2, 3, 8, PTS), F32),
                 pltpu.VMEM((2, 2, n_side * n_side, n_gx, 8, PTS), BF16),
                 pltpu.VMEM((PAD * PTS, 32), BF16),
-                pltpu.VMEM((32, LEAF_DEV * PTS), BF16),
+                pltpu.VMEM((32, (HALO + LEAF_DEV) * PTS), BF16),
                 pltpu.VMEM((32 * PAD, PTS), F32),
                 pltpu.VMEM((8 * PAIRS, SPAN), F32),
                 pltpu.VMEM((8, PAD * PTS), F32),
-                pltpu.VMEM((PAIRS, SPAN, 256), BF16),
+                pltpu.VMEM((PAIRS + SIDE, UPPER, 256), BF16),
                 pltpu.VMEM((16, INTER), jnp.int32),
                 pltpu.VMEM((16, INTER), jnp.int32),
                 pltpu.VMEM((12 * OPS, cols), BF16),
                 pltpu.VMEM((32 * OPS, PTS), F32),
                 pltpu.VMEM((LEAF_DEV, PTS), F32),
                 pltpu.VMEM((OPS, NODES, NODES), BF16),
+                pltpu.VMEM((cols, INTER), jnp.int16),
                 dma, dma((2,)), dma((2,)), dma((2, 2)), dma((2, 2)), dma((4,)), dma((4,)), dma((2, 3)), dma((2, 3)),
-                dma((2, n_gx - 1)), dma((2, n_gx - 1)), dma((2, n_side - 1)), dma((2, n_side - 1)),
-                dma((2, n_side - 1, n_side)), dma((2, n_side - 1, n_side)), dma((2, n_side, n_side)), dma((2, n_side, n_side)),
+                dma((2, n_gx - 1)), dma((2, n_gx - 1)),
+                dma((2, n_side, n_side)), dma((2, n_side, n_side)), dma((2, n_side, n_side)), dma((2, n_side, n_side)),
             ],
             compiler_params=pltpu.CompilerParams(
                 collective_id=0, has_side_effects=True, vmem_limit_bytes=60 * 1024 * 1024

time: 65.4 us -> 60.9 us (0.931)
  Pallas kernels: 63.2 us -> 58.7 us
    pallas_call x1, Pallas kernels: 63.2 us -> 58.7 us  [shards(): pl.pallas_call(functools.partial(kernel, sizes), out_shape=jax.ShapeDtype...]
where the time goes in v3:
time: 60.9 us; the launch traced here: 60.7 us
  Pallas kernels  58.7 us (96%)
  local copies, waits for them, and re-layouts  1.35 us (2%)
  between operations  0.64 us (1%)
    pallas_call x1, Pallas kernels, shards(): pl.pallas_call(functools.partial(kernel, sizes), out_shape=jax.ShapeDtype...  58.7 us
    squeeze x1, local copies, waits for them, and re-layouts, shards(): return (out[0], out[1])  1.35 us

profile of v3, /device:TPU:1, one launch (start us, length us, event | category | flops | bytes accessed | tf_op | source)
XLA Modules:
  0.0 60.7 jit_solution(11658822471328754059)
XLA Ops:
  0.6 58.7 %shard_map.122 = f32[2,32,128]{2,1,0:T(8,128)} custom-call(f32[3,32,128]{2,1,0:T(8,128)} %bitcast.5, f32[32,128]{1,0:T(8,128)} %source.1, f32[32,128]{1,0:T(8,128)} %density.1, bf16[32,216,128]{2,1,0:T(8,128)(2,1)} %anterp.1, s32[32]{0:T(128)} %child_slot.1, bf16[8,216,216]{2,1,0:T(8,128)(2,1)} %child_ops.1, s32[32]{0:T(128)} %parent.1, s32[32,27]{1,0:T(8,128)} %near_list.1, ...), custom_call_target="tpu_custom_call" | custom-call | tf_op jit(solution)/shard_map/pallas_call | solution.py:456
  59.4 1.3 %slice_bitcast_fusion = (f32[32,128]{1,0:T(8,128)}, f32[32,128]{1,0:T(8,128)}) fusion(f32[2,32,128]{2,1,0:T(8,128)} %shard_map.122), kind=kLoop, calls=%fused_computation | loop fusion | bytes 65536 | tf_op jit(solution)/shard_map/squeeze | solution.py:492

commit v4 on v3

--- a/solution.py
+++ b/solution.py
@@ -56,11 +56,12 @@
 
 def kernel(
     sizes,
-    points, source, density, anterp, child_slot, child_ops, parent, near_list, far_list, far_op, translations,
+    points_hbm, source_hbm, density_hbm, anterp_hbm, child_slot_hbm, child_ops_hbm, parent_hbm, near_list_hbm, far_list_hbm, far_op_hbm, translations_hbm,
     result,
     pts_pad, q_pad, fl_prev, fl_next, fo_prev, fo_next, part_out, part_in, table,
     src_feat, tgt_feat, feat, mask_wide, q_wide, kmat, codes, ops, counts, grouped, near, trans, rows_of,
-    tr_sem, pt_ss, pt_rs, q_ss, q_rs, li_ss, li_rs, pa_ss, pa_rs, z_ss, z_rs, a_ss, a_rs, c_ss, c_rs,
+    points, source, density, anterp, child_slot, child_ops, parent, near_list, far_list, far_op,
+    load_sem, tr_sem, pt_ss, pt_rs, q_ss, q_rs, li_ss, li_rs, pa_ss, pa_rs, z_ss, z_rs, a_ss, a_rs, c_ss, c_rs,
 ):
     n_gx, n_gy, n_gz = sizes
     n_x = n_gz // 2
@@ -98,8 +99,22 @@
     for peer in peers:
         pl.semaphore_signal(barrier, inc=1, device_id=peer, device_id_type=MESH)
 
-    load_trans = pltpu.make_async_copy(translations, trans, tr_sem)
+    loads = [
+        pltpu.make_async_copy(src, dst, load_sem.at[k])
+        for k, (src, dst) in enumerate(
+            (
+                (density_hbm, density), (parent_hbm, parent), (child_slot_hbm, child_slot), (near_list_hbm, near_list),
+                (points_hbm, points), (far_list_hbm, far_list), (far_op_hbm, far_op), (source_hbm, source),
+                (anterp_hbm, anterp), (child_ops_hbm, child_ops),
+            )
+        )
+    ]
+    for load in loads:
+        load.start()
+    load_trans = pltpu.make_async_copy(translations_hbm, trans, tr_sem)
     load_trans.start()
+    for load in loads[:3]:
+        load.wait()
     pslot = parent[...].reshape(1, LEAF_DEV) - (device * OCT_DEV - OCT_DEV)
     cslot = child_slot[...].reshape(1, LEAF_DEV)
     square = iota((LEAF_DEV, LEAF_DEV), 0) == iota((LEAF_DEV, LEAF_DEV), 1)
@@ -215,15 +230,15 @@
         for copy in copies:
             copy.wait_send()
 
-    def planes(rows, values):
+    def planes(lo, hi, values):
         for f, value in enumerate(values):
-            feat[f * PAD : f * PAD + rows, :] = value
+            feat[f * PAD + lo : f * PAD + hi, :] = value
 
     def build_source():
         parts = [split3(pts_pad[c]) for c in range(3)]
         norm = split3(pts_pad[0] * pts_pad[0] + pts_pad[1] * pts_pad[1] + pts_pad[2] * pts_pad[2])
         values = [parts[c][k] for k in (0, 0, 1, 1, 0, 2) for c in range(3)] + list(norm) + [jnp.ones((PAD, PTS), F32)] * 3
-        planes(PAD, values)
+        planes(0, PAD, values)
 
         def body(w, carry):
             tile = jnp.transpose(feat[pl.ds(w, 32, stride=PAD), :]).astype(BF16)
@@ -232,18 +247,18 @@
 
         lax.fori_loop(2, PAD - 2, body, 0, unroll=4)
 
-    def build_target():
-        parts = [[-2.0 * v for v in split3(pts_pad[c])] for c in range(3)]
-        norm = split3(pts_pad[0] * pts_pad[0] + pts_pad[1] * pts_pad[1] + pts_pad[2] * pts_pad[2] + SOFTEN)
-        values = [parts[c][k] for k in (0, 1, 0, 1, 2, 0) for c in range(3)] + [jnp.ones((PAD, PTS), F32)] * 3 + list(norm)
-        planes(PAD, values)
-        feat[24 * PAD :, :] = jnp.zeros((8 * PAD, PTS), F32)
+    def build_target(lo, hi):
+        pts = [pts_pad[c, lo:hi] for c in range(3)]
+        parts = [[-2.0 * v for v in split3(p)] for p in pts]
+        norm = split3(pts[0] * pts[0] + pts[1] * pts[1] + pts[2] * pts[2] + SOFTEN)
+        values = [parts[c][k] for k in (0, 1, 0, 1, 2, 0) for c in range(3)]
+        planes(lo, hi, values + [jnp.ones((hi - lo, PTS), F32)] * 3 + list(norm))
 
         def body(w, carry):
             tgt_feat[:, pl.ds(pl.multiple_of(w * PTS, PTS), PTS)] = feat[pl.ds(w, 32, stride=PAD), :].astype(BF16)
             return carry
 
-        lax.fori_loop(0, HALO + LEAF_DEV, body, 0, unroll=6)
+        lax.fori_loop(lo, hi, body, 0, unroll=8)
 
     def build_mask():
         listed = near_list[...]
@@ -376,6 +391,12 @@
     first, last = pl.ds(0, HALO), pl.ds(HALO, HALO)
     after = pl.ds(HALO + LEAF_DEV, HALO)
     q_pad[0, HALO : HALO + LEAF_DEV, :] = density[...]
+    for load in loads[3:8]:
+        load.wait()
+    feat[24 * PAD :, :] = jnp.zeros((8 * PAD, PTS), F32)
+    build_mask()
+    for load in loads[8:]:
+        load.wait()
     partial(0, density[...])
     pl.semaphore_wait(barrier, len(peers))
     sent = send_partial(0)
@@ -397,12 +418,12 @@
     sent = sent + halo + lists
     for c in range(3):
         pts_pad[c, HALO : HALO + LEAF_DEV, :] = points[c]
-    build_mask()
+    build_target(HALO, HALO + LEAF_DEV)
     own_multipole(0)
     copies = send_z(0)
     sent = sent + copies
     arrive(halo)
-    build_target()
+    build_target(0, HALO)
     build_source()
     build_halo()
     build_q(0)
@@ -456,7 +477,7 @@
         out = pl.pallas_call(
             functools.partial(kernel, sizes),
             out_shape=jax.ShapeDtypeStruct((2, LEAF_DEV, PTS), F32),
-            in_specs=[vmem] * 10 + [pl.BlockSpec(memory_space=pl.ANY)],
+            in_specs=[pl.BlockSpec(memory_space=pl.ANY)] * 11,
             out_specs=vmem,
             scratch_shapes=[
                 pltpu.VMEM((3, PAD, PTS), F32),
@@ -481,7 +502,17 @@
                 pltpu.VMEM((LEAF_DEV, PTS), F32),
                 pltpu.VMEM((OPS, NODES, NODES), BF16),
                 pltpu.VMEM((cols, INTER), jnp.int16),
-                dma, dma((2,)), dma((2,)), dma((2, 2)), dma((2, 2)), dma((4,)), dma((4,)), dma((2, 3)), dma((2, 3)),
+                pltpu.VMEM((3, LEAF_DEV, PTS), F32),
+                pltpu.VMEM((LEAF_DEV, PTS), F32),
+                pltpu.VMEM((LEAF_DEV, PTS), F32),
+                pltpu.VMEM((LEAF_DEV, NODES, PTS), BF16),
+                pltpu.VMEM((LEAF_DEV,), jnp.int32),
+                pltpu.VMEM((8, NODES, NODES), BF16),
+                pltpu.VMEM((LEAF_DEV,), jnp.int32),
+                pltpu.VMEM((LEAF_DEV, NEAR), jnp.int32),
+                pltpu.VMEM((OCT_DEV, INTER), jnp.int32),
+                pltpu.VMEM((OCT_DEV, INTER), jnp.int32),
+                dma((10,)), dma, dma((2,)), dma((2,)), dma((2, 2)), dma((2, 2)), dma((4,)), dma((4,)), dma((2, 3)), dma((2, 3)),
                 dma((2, n_gx - 1)), dma((2, n_gx - 1)),
                 dma((2, n_side, n_side)), dma((2, n_side, n_side)), dma((2, n_side, n_side)), dma((2, n_side, n_side)),
             ],

time: 60.9 us -> 59.6 us (0.979)
  Pallas kernels: 58.7 us -> 57.3 us
    pallas_call x1, Pallas kernels: 58.7 us -> 57.3 us  [shards(): pl.pallas_call(functools.partial(kernel, sizes), out_shape=jax.ShapeDtype...]
where the time goes in v4:
time: 59.6 us; the launch traced here: 59.3 us
  Pallas kernels  57.3 us (96%)
  local copies, waits for them, and re-layouts  1.35 us (2%)
  between operations  0.64 us (1%)
    pallas_call x1, Pallas kernels, shards(): pl.pallas_call(functools.partial(kernel, sizes), out_shape=jax.ShapeDtype...  57.3 us
    squeeze x1, local copies, waits for them, and re-layouts, shards(): return (out[0], out[1])  1.35 us

profile of v4, /device:TPU:1, one launch (start us, length us, event | category | flops | bytes accessed | tf_op | source)
XLA Modules:
  0.0 59.3 jit_solution(4069892719906381923)
XLA Ops:
  0.6 57.3 %shard_map.122 = f32[2,32,128]{2,1,0:T(8,128)} custom-call(f32[3,32,128]{2,1,0:T(8,128)} %bitcast.5, f32[32,128]{1,0:T(8,128)} %source_hbm.1, f32[32,128]{1,0:T(8,128)} %density_hbm.1, bf16[32,216,128]{2,1,0:T(8,128)(2,1)} %anterp_hbm.1, s32[32]{0:T(128)} %child_slot_hbm.1, bf16[8,216,216]{2,1,0:T(8,128)(2,1)} %child_ops_hbm.1, s32[32]{0:T(128)} %parent_hbm.1, ...), custom_call_target="tpu_custom_call" | custom-call | tf_op jit(solution)/shard_map/pallas_call | solution.py:477
  58.0 1.3 %slice_bitcast_fusion = (f32[32,128]{1,0:T(8,128)}, f32[32,128]{1,0:T(8,128)}) fusion(f32[2,32,128]{2,1,0:T(8,128)} %shard_map.122), kind=kLoop, calls=%fused_computation | loop fusion | bytes 65536 | tf_op jit(solution)/shard_map/squeeze | solution.py:523

commit v5 on v4

--- a/solution.py
+++ b/solution.py
@@ -446,7 +446,8 @@
     q_pad[1, HALO : HALO + LEAF_DEV, :] = q
     halo = send_q(1, q_pad.at[1, own])
     partial(1, q)
-    sent = sent + halo + send_partial(1)
+    earlier = sent
+    sent = halo + send_partial(1)
     arrive(halo)
     build_q(1)
     own_multipole(1)
@@ -456,6 +457,7 @@
     arrive(copies)
     sent = sent + gather_start(1)
     near_again(PAIRS // 2, PAIRS)
+    left(earlier)
     sent = sent + gather_middle(1)
     sent = sent + gather_end(1)
     potential = FAR_WEIGHT * far_field(1) + NEAR_WEIGHT * near[...]

time: 59.6 us -> 59.5 us (level)
  no operation moved by 1% of the time
where the time goes in v5:
time: 59.5 us; the launch traced here: 59.3 us
  Pallas kernels  57.3 us (96%)
  local copies, waits for them, and re-layouts  1.35 us (2%)
  between operations  0.64 us (1%)
    pallas_call x1, Pallas kernels, shards(): pl.pallas_call(functools.partial(kernel, sizes), out_shape=jax.ShapeDtype...  57.3 us
    squeeze x1, local copies, waits for them, and re-layouts, shards(): return (out[0], out[1])  1.35 us

profile of v5, /device:TPU:1, one launch (start us, length us, event | category | flops | bytes accessed | tf_op | source)
XLA Modules:
  0.0 59.3 jit_solution(11608156995131831705)
XLA Ops:
  0.6 57.3 %shard_map.122 = f32[2,32,128]{2,1,0:T(8,128)} custom-call(f32[3,32,128]{2,1,0:T(8,128)} %bitcast.5, f32[32,128]{1,0:T(8,128)} %source_hbm.1, f32[32,128]{1,0:T(8,128)} %density_hbm.1, bf16[32,216,128]{2,1,0:T(8,128)(2,1)} %anterp_hbm.1, s32[32]{0:T(128)} %child_slot_hbm.1, bf16[8,216,216]{2,1,0:T(8,128)(2,1)} %child_ops_hbm.1, s32[32]{0:T(128)} %parent_hbm.1, ...), custom_call_target="tpu_custom_call" | custom-call | tf_op jit(solution)/shard_map/pallas_call | solution.py:479
  57.9 1.3 %slice_bitcast_fusion = (f32[32,128]{1,0:T(8,128)}, f32[32,128]{1,0:T(8,128)}) fusion(f32[2,32,128]{2,1,0:T(8,128)} %shard_map.122), kind=kLoop, calls=%fused_computation | loop fusion | bytes 65536 | tf_op jit(solution)/shard_map/squeeze | solution.py:525
